TPU v7x, 32 devices: a whole 2x2x4 slice. The times are simulated.
32 devices in a mesh: bucket: 16 (over z, y, x), seq: 2 (over core).
Axes of the slice: x: 2, y: 2, z: 4, core: 2. Of those that a mesh axis runs over, the one named last changes fastest.
Arguments:
- tokens: bfloat16 [64, 512, 384], P('bucket', 'seq'), may hold values from -6 to 6
- cotangent: bfloat16 [64, 512, 384], P('bucket', 'seq'), may hold values from -6 to 6
- segment_ids: int32 [64, 512], P('bucket'), may hold values from 0 to 7, never falling along the last dimension, each value on 1 to 256 neighbouring positions
- pad_counts: int32 [64], P('bucket'), may hold values from 0 to 128
- timesteps: int32 [64, 8], P('bucket'), may hold values from 0 to 999
- classes: int32 [64, 8], P('bucket'), may hold values from 0 to 999
- head_mask: int32 [64, 8, 6], P('bucket'), may hold values 0 or 1
- channel_mask: int32 [64, 8, 24], P('bucket'), may hold values 0 or 1
- keep_mask: int32 [64, 512], P('bucket', 'seq'), may hold values 0 or 1
- class_table: bfloat16 [1000, 384], replicated, may hold values from -6 to 6
- w_ada: bfloat16 [384, 2304], P('bucket', 'seq'), may hold values from -0.3125 to 0.3125
- b_ada: bfloat16 [2304], P('seq'), may hold values from -2 to 2
- w_qkv: bfloat16 [384, 1152], replicated, may hold values from -0.3125 to 0.3125
- bias_qv: bfloat16 [768], replicated, may hold values from -2 to 2
- w_proj: bfloat16 [384, 384], replicated, may hold values from -2.5 to 2.5
- b_proj: bfloat16 [384], replicated, may hold values from -2 to 2
- w_fc1: bfloat16 [384, 1536], replicated, may hold values from -0.3125 to 0.3125
- b_fc1: bfloat16 [1536], replicated, may hold values from -2 to 2
- w_fc2: bfloat16 [1536, 384], replicated, may hold values from -0.15625 to 0.15625
- b_fc2: bfloat16 [384], replicated, may hold values from -2 to 2
- w_router: bfloat16 [384], replicated, may hold values from -0.3125 to 0.3125
Outputs:
- output: bfloat16 [64, 512, 384], P('bucket', 'seq')
- grad_tokens: bfloat16 [64, 512, 384], P('bucket', 'seq')
- grad_class_table: float32 [1000, 384], P(None, 'bucket')
- grad_w_ada: float32 [384, 2304], P('bucket', 'seq')
- grad_b_ada: float32 [2, 1152], P('seq', 'bucket')
- grad_w_qkv: float32 [384, 1152], P(None, 'bucket')
- grad_bias_qv: float32 [768], P('bucket')
- grad_w_proj: float32 [384, 384], P(None, 'bucket')
- grad_b_proj: float32 [384], P('bucket')
- grad_w_fc1: float32 [384, 1536], P(None, 'bucket')
- grad_b_fc1: float32 [1536], P('bucket')
- grad_w_fc2: float32 [1536, 384], P('bucket')
- grad_b_fc2: float32 [384], P('bucket')
- grad_w_router: float32 [384], P('bucket')
Inputs may be any that keep to these rules, and one draw needn't show every extreme that they name: `segment_ids`: crop numbers never fall along a row; each crop has 1 to 256 tokens and one has exactly 256. The padding tokens are the last pad_counts[r] tokens of row r.
All inputs are finite; a program needn't handle non-finite values. No bound on the sum of `head_mask` or of `channel_mask` or of `keep_mask` on one device may be relied on, other than what follows from the above.
Results may differ from a plain program's by a relative error of at most 0.014.
The roundings to bfloat16 on the way count: a program that leaves them out, or rounds other values in their place, can miss the bound.
Values may be sent and summed in bfloat16 or wider, within the bound.
No kernel may reach another device: no remote copies, remote signals or barrier semaphores. Data moves between devices by JAX's collectives and lax.ppermute only.
A program may use at most 192 MiB of HBM per device.

v0:
```python
from functools import partial
import math

import jax
import jax.numpy as jnp
from jax import lax
from jax.sharding import PartitionSpec as P

D = 384
HEADS = 6
HEAD_DIM = 64
FF = 1536
NCLASS = 1000
CGROUPS = 24
CROPS = 8


HIGHEST_PRECISION = lax.Precision.HIGHEST
EPSILON = 1e-06
NEGATIVE = -1e30


def exact(form, left, right):
    return jnp.einsum(form, left, right, precision=HIGHEST_PRECISION)


def layer_norm(values_in):
    centred = values_in - jnp.mean(values_in, -1, keepdims=True)
    variance = jnp.mean(centred * centred, -1, keepdims=True)
    return centred * lax.rsqrt(variance + EPSILON)


def time_embed(timesteps):
    half_width = D // 2
    frequency = jnp.exp(-math.log(10000.0) * jnp.arange(half_width, dtype=jnp.float32) / half_width)
    angles = timesteps.astype(jnp.float32)[..., None] * frequency
    return jnp.concatenate([jnp.cos(angles), jnp.sin(angles)], -1)


def first_norm(token_in, shift_in, scale_in):
    return layer_norm(token_in) * (1.0 + scale_in) + shift_in


def heads_view(matrix):
    return matrix.reshape(matrix.shape[0], HEADS, HEAD_DIM)


def body(
    tokens,
    cotangent,
    segment_ids,
    pad_counts,
    timesteps,
    classes,
    head_mask,
    channel_mask,
    keep_mask,
    class_table,
    w_ada,
    b_ada,
    w_qkv,
    bias_qv,
    w_proj,
    b_proj,
    w_fc1,
    b_fc1,
    w_fc2,
    b_fc2,
    w_router,
):
    row_count, local_len, width_all = tokens.shape
    full_len = local_len * lax.axis_size("seq")
    first_pos = lax.axis_index("seq") * local_len
    token_count = row_count * local_len
    shape_three = (row_count, local_len, D)
    position = jnp.arange(full_len, dtype=jnp.int32)
    live_row = position[None, :] < (full_len - pad_counts)[:, None]
    attend_keys = jnp.where(live_row, segment_ids, -1)
    attend_query = lax.dynamic_slice_in_dim(attend_keys, first_pos, local_len, 1)
    live_here = lax.dynamic_slice_in_dim(live_row.astype(jnp.float32), first_pos, local_len, 1)
    crop_here = lax.dynamic_slice_in_dim(segment_ids, first_pos, local_len, 1)
    crop_hot = (crop_here[:, :, None] == jnp.arange(CROPS, dtype=jnp.int32)).astype(jnp.float32)
    class_hot = (classes[:, :, None] == jnp.arange(NCLASS, dtype=jnp.int32)).astype(jnp.float32)
    ada_full = lax.all_gather(w_ada, "bucket", axis=0, tiled=True)
    condition = time_embed(timesteps) + exact(
        "rcn,nd->rcd", class_hot, class_table.astype(jnp.float32)
    )
    silu_value, pull_silu = jax.vjp(jax.nn.silu, condition)
    silu_low = silu_value.astype(jnp.bfloat16)
    mod_part = jnp.einsum(
        "rcd,dm->rcm", silu_low, ada_full, preferred_element_type=jnp.float32
    ) + b_ada.astype(jnp.float32)
    modulation = lax.all_gather(mod_part, "seq", axis=2, tiled=True)
    per_token = exact("rlc,rcm->rlm", crop_hot, modulation)
    shift_one, scale_one, gate_one, shift_two, scale_two, gate_two = jnp.split(
        per_token, 6, axis=-1
    )
    token_float = tokens.astype(jnp.float32)
    hidden_one, pull_first = jax.vjp(first_norm, token_float, shift_one, scale_one)
    hidden_low = hidden_one.astype(jnp.bfloat16).reshape(token_count, D)
    projected = jnp.dot(hidden_low, w_qkv, preferred_element_type=jnp.float32)
    bias_float = bias_qv.astype(jnp.float32)
    query = (projected[:, :D] + bias_float[:D]).astype(jnp.bfloat16).reshape(shape_three)
    key_here = projected[:, D : 2 * D].astype(jnp.bfloat16).reshape(shape_three)
    value_here = (projected[:, 2 * D :] + bias_float[D:]).astype(jnp.bfloat16).reshape(shape_three)
    key_rows, value_rows = (
        lax.all_gather(key_here, "seq", axis=1, tiled=True),
        lax.all_gather(value_here, "seq", axis=1, tiled=True),
    )
    same_crop = attend_query[:, :, None] == attend_keys[:, None, :]
    score_scale = HEAD_DIM ** (-0.5)

    def raw_scores(query_row, key_row, same_row):
        scores = (
            jnp.einsum(
                "qhe,khe->hqk",
                heads_view(query_row),
                heads_view(key_row),
                preferred_element_type=jnp.float32,
            )
            * score_scale
        )
        return jnp.where(same_row[None], scores, NEGATIVE)

    def attend(item):
        query_row, key_row, value_row, same_row = item
        scores = raw_scores(query_row, key_row, same_row)
        row_max = jnp.max(scores, -1, keepdims=True)
        numerator = jnp.exp(scores - row_max)
        denominator = jnp.sum(numerator, -1, keepdims=True)
        probability = (numerator / denominator).astype(jnp.bfloat16)
        mixed_heads = jnp.einsum(
            "hqk,khe->qhe", probability, heads_view(value_row), preferred_element_type=jnp.float32
        )
        return (mixed_heads, (row_max + jnp.log(denominator))[..., 0])

    mixed_heads, log_total = lax.map(attend, (query, key_rows, value_rows, same_crop))
    head_scale = exact("rlc,rch->rlh", crop_hot, head_mask.astype(jnp.float32))[..., None]
    attended = (mixed_heads * head_scale).astype(jnp.bfloat16).reshape(token_count, D)
    branch = (
        jnp.dot(attended, w_proj, preferred_element_type=jnp.float32) + b_proj.astype(jnp.float32)
    ).reshape(shape_three)
    live_column = live_here[..., None]

    def second_norm(token_in, branch_in, gate_in, shift_in, scale_in):
        residual_in = token_in + live_column * gate_in * branch_in
        return (residual_in, layer_norm(residual_in) * (1.0 + scale_in) + shift_in)

    (residual, hidden_two), pull_second = jax.vjp(
        second_norm, token_float, branch, gate_one, shift_two, scale_two
    )
    second_low = hidden_two.astype(jnp.bfloat16).reshape(token_count, D)
    router_rate = jax.nn.sigmoid(jnp.dot(second_low, w_router, preferred_element_type=jnp.float32))
    pre_act = jnp.dot(second_low, w_fc1, preferred_element_type=jnp.float32) + b_fc1.astype(
        jnp.float32
    )
    chans_tok = exact(
        "rlc,rcf->rlf",
        crop_hot,
        jnp.repeat(channel_mask.astype(jnp.float32), FF // CGROUPS, axis=-1),
    ).reshape(token_count, FF)
    gelu_out, pull_gelu = jax.vjp(partial(jax.nn.gelu, approximate=True), pre_act)
    activation = (gelu_out * chans_tok).astype(jnp.bfloat16)
    mlp_out = jnp.dot(activation, w_fc2, preferred_element_type=jnp.float32) + b_fc2.astype(
        jnp.float32
    )
    keep_live = (live_here * keep_mask.astype(jnp.float32)).reshape(token_count)
    branch_coef = keep_live * router_rate
    gate_flat = gate_two.reshape(token_count, D)
    outcome = residual.reshape(token_count, D) + branch_coef[:, None] * gate_flat * mlp_out
    output = outcome.astype(jnp.bfloat16).reshape(shape_three)
    grad_out = cotangent.astype(jnp.float32).reshape(token_count, D)
    grad_mlp = (grad_out * branch_coef[:, None] * gate_flat).astype(jnp.bfloat16)
    grad_gate_two = grad_out * branch_coef[:, None] * mlp_out
    grad_rate = jnp.sum(grad_out * gate_flat * mlp_out, -1) * keep_live
    grad_logit = grad_rate * router_rate * (1.0 - router_rate)
    grad_w_fc2 = jnp.einsum("nf,nd->fd", activation, grad_mlp, preferred_element_type=jnp.float32)
    grad_b_fc2 = jnp.sum(grad_mlp.astype(jnp.float32), 0)
    grad_act = jnp.einsum("nd,fd->nf", grad_mlp, w_fc2, preferred_element_type=jnp.float32)
    grad_pre = pull_gelu(grad_act * chans_tok)[0].astype(jnp.bfloat16)
    grad_w_fc1 = jnp.einsum("nd,nf->df", second_low, grad_pre, preferred_element_type=jnp.float32)
    grad_b_fc1 = jnp.sum(grad_pre.astype(jnp.float32), 0)
    grad_w_router = exact("nd,n->d", second_low.astype(jnp.float32), grad_logit)
    grad_hidden_two = (
        jnp.einsum("nf,df->nd", grad_pre, w_fc1, preferred_element_type=jnp.float32)
        + grad_logit[:, None] * w_router.astype(jnp.float32)[None, :]
    )
    part_fc1, part_bfc1, part_fc2, part_bfc2, part_router = (
        lax.psum_scatter(grad_w_fc1, "bucket", scatter_dimension=1, tiled=True),
        lax.psum_scatter(grad_b_fc1, "bucket", scatter_dimension=0, tiled=True),
        lax.psum_scatter(grad_w_fc2, "bucket", scatter_dimension=0, tiled=True),
        lax.psum_scatter(grad_b_fc2, "bucket", scatter_dimension=0, tiled=True),
        lax.psum_scatter(grad_w_router, "bucket", scatter_dimension=0, tiled=True),
    )
    mlp_sums = (
        lax.psum(part_fc1.astype(jnp.bfloat16), "seq").astype(jnp.float32),
        lax.psum(part_bfc1.astype(jnp.bfloat16), "seq").astype(jnp.float32),
        lax.psum(part_fc2.astype(jnp.bfloat16), "seq").astype(jnp.float32),
        lax.psum(part_bfc2.astype(jnp.bfloat16), "seq").astype(jnp.float32),
        lax.psum(part_router.astype(jnp.bfloat16), "seq").astype(jnp.float32),
    )
    grad_token_one, grad_branch, grad_gate_one, grad_shift_two, grad_scale_two = pull_second(
        (grad_out.reshape(shape_three), grad_hidden_two.reshape(shape_three))
    )
    branch_low = grad_branch.astype(jnp.bfloat16).reshape(token_count, D)
    grad_w_proj = jnp.einsum("nd,ne->de", attended, branch_low, preferred_element_type=jnp.float32)
    grad_b_proj = jnp.sum(branch_low.astype(jnp.float32), 0)
    grad_attended = jnp.einsum(
        "ne,de->nd", branch_low, w_proj, preferred_element_type=jnp.float32
    ).astype(jnp.bfloat16)
    grad_heads = grad_attended.reshape(row_count, local_len, HEADS, HEAD_DIM) * head_scale.astype(
        jnp.bfloat16
    )

    def attend_back(item):
        query_row, key_row, value_row, same_row, total_row, grad_row = item
        scores = raw_scores(query_row, key_row, same_row)
        probability = jnp.exp(scores - total_row[..., None])
        grad_prob = jnp.einsum(
            "qhe,khe->hqk", grad_row, heads_view(value_row), preferred_element_type=jnp.float32
        )
        inner = jnp.sum(probability * grad_prob, -1)
        grad_scores = (probability * (grad_prob - inner[..., None])).astype(jnp.bfloat16)
        grad_query = (
            jnp.einsum(
                "hqk,khe->qhe", grad_scores, heads_view(key_row), preferred_element_type=jnp.float32
            )
            * score_scale
        ).astype(jnp.bfloat16)
        return (grad_query.reshape(-1, D), inner)

    grad_query, inner_total = lax.map(
        attend_back, (query, key_rows, value_rows, same_crop, log_total, grad_heads)
    )
    query_all, grad_heads_all = (
        lax.all_gather(query, "seq", axis=1, tiled=True),
        lax.all_gather(grad_heads, "seq", axis=1, tiled=True),
    )
    total_all, inner_all = (
        lax.all_gather(log_total, "seq", axis=2, tiled=True),
        lax.all_gather(inner_total, "seq", axis=2, tiled=True),
    )
    same_owner = attend_keys[:, :, None] == attend_query[:, None, :]

    def owner_back(item):
        query_row, key_row, value_row, same_row, total_row, inner_row, grad_row = item
        scores = raw_scores(query_row, key_row, same_row)
        probability = jnp.exp(scores - total_row[..., None])
        grad_prob = jnp.einsum(
            "qhe,khe->hqk", grad_row, heads_view(value_row), preferred_element_type=jnp.float32
        )
        grad_scores = (probability * (grad_prob - inner_row[..., None])).astype(jnp.bfloat16)
        grad_key = (
            jnp.einsum(
                "hqk,qhe->khe",
                grad_scores,
                heads_view(query_row),
                preferred_element_type=jnp.float32,
            )
            * score_scale
        ).astype(jnp.bfloat16)
        grad_value = jnp.einsum(
            "hqk,qhe->khe",
            probability.astype(jnp.bfloat16),
            grad_row,
            preferred_element_type=jnp.float32,
        ).astype(jnp.bfloat16)
        return (grad_key.reshape(-1, D), grad_value.reshape(-1, D))

    key_grad, value_grad = lax.map(
        owner_back,
        (query_all, key_here, value_here, same_owner, total_all, inner_all, grad_heads_all),
    )
    grad_projected = jnp.concatenate([grad_query, key_grad, value_grad], -1).reshape(
        token_count, 3 * D
    )
    grad_w_qkv = jnp.einsum(
        "nd,ne->de", hidden_low, grad_projected, preferred_element_type=jnp.float32
    )
    grad_bias_qv = jnp.concatenate(
        [
            jnp.sum(grad_projected[:, :D].astype(jnp.float32), 0),
            jnp.sum(grad_projected[:, 2 * D :].astype(jnp.float32), 0),
        ]
    )
    grad_hidden_one = jnp.einsum(
        "ne,de->nd", grad_projected, w_qkv, preferred_element_type=jnp.float32
    ).reshape(shape_three)
    grad_token_two, grad_shift_one, grad_scale_one = pull_first(grad_hidden_one)
    grad_tokens = (grad_token_one + grad_token_two).astype(jnp.bfloat16)
    grad_per_token = jnp.concatenate(
        [
            grad_shift_one,
            grad_scale_one,
            grad_gate_one,
            grad_shift_two,
            grad_scale_two,
            grad_gate_two.reshape(shape_three),
        ],
        -1,
    )
    mod_parts = exact("rlc,rlm->rcm", crop_hot, grad_per_token)
    grad_mod = lax.psum_scatter(
        mod_parts.astype(jnp.bfloat16), "seq", scatter_dimension=2, tiled=True
    )
    grad_w_ada = jnp.einsum("rcd,rcm->dm", silu_low, grad_mod, preferred_element_type=jnp.float32)
    grad_b_ada = jnp.sum(grad_mod.astype(jnp.float32), (0, 1))
    grad_silu = jnp.einsum("rcm,dm->rcd", grad_mod, ada_full, preferred_element_type=jnp.float32)
    grad_condition = pull_silu(grad_silu)[0]
    grad_table = exact("rcn,rcd->nd", class_hot, grad_condition)
    bucket_count = lax.axis_size("bucket")
    grad_w_ada, grad_b_ada = (
        lax.psum_scatter(grad_w_ada, "bucket", scatter_dimension=0, tiled=True),
        lax.psum_scatter(
            grad_b_ada.reshape(bucket_count, -1), "bucket", scatter_dimension=0, tiled=True
        ),
    )
    part_table, part_qkv, part_bias_qv, part_proj, part_bproj = (
        lax.psum_scatter(grad_table, "bucket", scatter_dimension=1, tiled=True),
        lax.psum_scatter(grad_w_qkv, "bucket", scatter_dimension=1, tiled=True),
        lax.psum_scatter(grad_bias_qv, "bucket", scatter_dimension=0, tiled=True),
        lax.psum_scatter(grad_w_proj, "bucket", scatter_dimension=1, tiled=True),
        lax.psum_scatter(grad_b_proj, "bucket", scatter_dimension=0, tiled=True),
    )
    attention_sums = (
        lax.psum(part_table.astype(jnp.bfloat16), "seq").astype(jnp.float32),
        lax.psum(part_qkv.astype(jnp.bfloat16), "seq").astype(jnp.float32),
        lax.psum(part_bias_qv.astype(jnp.bfloat16), "seq").astype(jnp.float32),
        lax.psum(part_proj.astype(jnp.bfloat16), "seq").astype(jnp.float32),
        lax.psum(part_bproj.astype(jnp.bfloat16), "seq").astype(jnp.float32),
    )
    summed = tuple(attention_sums) + tuple(mlp_sums)
    return (
        output,
        grad_tokens,
        summed[0],
        grad_w_ada,
        grad_b_ada,
        summed[1],
        summed[2],
        summed[3],
        summed[4],
        summed[5],
        summed[6],
        summed[7],
        summed[8],
        summed[9],
    )


def solution(mesh):
    placed = (
        P("bucket", "seq", None),
        P("bucket", "seq", None),
        P("bucket", None),
        P("bucket"),
        P("bucket", None),
        P("bucket", None),
        P("bucket", None, None),
        P("bucket", None, None),
        P("bucket", "seq"),
        P(),
        P("bucket", "seq"),
        P("seq"),
        P(),
        P(),
        P(),
        P(),
        P(),
        P(),
        P(),
        P(),
        P(),
    )
    return jax.shard_map(
        body,
        mesh=mesh,
        in_specs=placed,
        out_specs=(
            P("bucket", "seq", None),
            P("bucket", "seq", None),
            P(None, "bucket"),
            P("bucket", "seq"),
            P("seq", "bucket"),
            P(None, "bucket"),
            P("bucket"),
            P(None, "bucket"),
            P("bucket"),
            P(None, "bucket"),
            P("bucket"),
            P("bucket", None),
            P("bucket"),
            P("bucket"),
        ),
        check_vma=False,
    )
```

profile of v0, /device:TPU:0, one launch (start us, length us, event | category | flops | bytes accessed | tf_op | source)
XLA Modules:
  0.0 1123.5 jit_solution(7249561307434286096)
XLA Ops:
  8.0 48.0 %all_gather.24 = bf16[384,1152]{1,0:T(8,128)(2,1)S(1)} all-gather(bf16[24,1152]{1,0:T(8,128)(2,1)} %param.37), channel_id=1, replica_groups=mesh['bucket'=16,'seq'=2] {'bucket'}, dimensions={0}, use_global_device_ids=true | all-gather | bytes 940032 | tf_op jit(solution)/shard_map/all_gather | solution.py:84
  62.3 6.3 fusion.91
  91.2 4.5 fusion.89
  95.7 19.8 %while.36 = (s32[]{:T(128)}, f32[4,256,6,64]{1,3,2,0:T(8,128)}, f32[4,6,256]{2,1,0:T(8,128)S(1)}, bf16[4,512,384]{1,2,0:T(8,128)(2,1)}, pred[4,256,512]{2,1,0:T(...) while((s32[]{:T(128)}, f32[4,256,6,64]{1,3,2,0:T(8,128)}, ...), condition=%wide.region_5.6_spmd, body=%wide.region_2.5_spmd.sunk | while | flops 210762240 | bytes 13490789 | solution.py:137
  125.6 3.5 fusion.47
  129.2 3.6 fusion.69
  132.9 7.4 convert_reduce_fusion
  155.4 23.7 %while.37 = (s32[]{:T(128)}, bf16[4,256,384]{2,1,0:T(8,128)(2,1)S(1)}, f32[4,6,256]{2,1,0:T(8,128)S(1)}, bf16[4,512,384]{1,2,0:T(8,128)(2,1)}, pred[4,256,512]{2...) while((s32[]{:T(128)}, ...), condition=%wide.region_13.14_spmd, body=%wide.region_11.13_spmd.sunk | while | flops 310835712 | bytes 20830336 | solution.py:232
  189.4 64.3 %while.38 = (s32[]{:T(128)}, bf16[4,256,384]{2,1,0:T(8,128)(2,1)}, bf16[4,256,384]{2,1,0:T(8,128)(2,1)}, bf16[4,512,384]{1,2,0:T(8,128)(2,1)}, pred[4,512,256]{2...) while((s32[]{:T(128)}, bf16[4,256,384]{2,1,0:T(8,128)(2,1)}, ...), condition=%wide.region_15.16_spmd, body=%wide.region_14.15_spmd.sunk | while | flops 410812416 | bytes 16132277 | solution.py:270
  200.6 3.2 fusion.198
  248.7 3.2 fusion.198
  257.1 4.6 convert_reduce_fusion.2
  282.7 5.1 fusion.112
  289.0 5.1 fusion.111
  300.2 4.3 convolution_bitcast_fusion
  308.2 108.3 %reduce-scatter.28.cloned.1.call-done = f32[384,24]{0,1:T(8,128)} async-done(((f32[384,384]{0,1:T(8,128)}), f32[384,24]{0,1:T(8,128)}) %reduce-scatter.28.cloned.1.call-update) | async-done | bytes 36880
  419.5 129.5 %reduce-scatter.20.cloned.1.call-done = f32[96,384]{1,0:T(8,128)} async-done(((f32[1536,384]{1,0:T(8,128)}), f32[96,384]{1,0:T(8,128)}) %reduce-scatter.20.cloned.1.call-update) | async-done | bytes 147472 | tf_op jit(solution)/shard_map/reduce_scatter | solution.py:191
  550.5 131.6 %reduce-scatter.18.cloned.1.call-done = f32[384,96]{0,1:T(8,128)} async-done(((f32[384,1536]{0,1:T(8,128)}), f32[384,96]{0,1:T(8,128)}) %reduce-scatter.18.cloned.1.call-update) | async-done | bytes 147472 | tf_op jit(solution)/shard_map/reduce_scatter | solution.py:189
  683.9 75.1 %all-reduce.9 = (f32[16,72]{1,0:T(8,128)S(1)}, bf16[768]{0:T(1024)(128)(2,1)S(1)}, bf16[384]{0:T(512)(128)(2,1)S(1)}, bf16[1536]{0:T(1024)(128)(2,1)S(1)}, bf16[...) all-reduce(f32[16,72]{1,0:T(8,128)S(1)} %reshape.261, ...), channel_id=5, replica_groups=mesh['bucket'=16,'seq'=2] {'bucket'}, use_global_device_ids=true, to_apply=%region_23.24.clone | all-reduce | flops 4608 | bytes 29952
  762.0 48.7 %reduce-scatter.16.cloned.1.call-done = f32[1000,24]{0,1:T(8,128)} async-done(((f32[1000,384]{0,1:T(8,128)}), f32[1000,24]{0,1:T(8,128)}) %reduce-scatter.16.cloned.1.call-update) | async-done | bytes 96016 | tf_op jit(solution)/shard_map/reduce_scatter | solution.py:319
  812.2 128.5 %reduce-scatter.26.cloned.1.call-done = f32[384,72]{0,1:T(8,128)} async-done(((f32[384,1152]{0,1:T(8,128)}), f32[384,72]{0,1:T(8,128)}) %reduce-scatter.26.cloned.1.call-update) | async-done | bytes 110608
  945.2 15.5 %all-reduce.17.cloned.1.call-done = (bf16[384,96]{0,1:T(8,128)(2,1)}, bf16[96,384]{1,0:T(8,128)(2,1)}) async-done(((bf16[384,96]{0,1:T(8,128)(2,1)}, bf16[96,384]{1,0:T(8,128)(2,1)}), (bf16[384,96]{0,1:T(8,128)(2,1)}, bf16[96,384]{1,0:T(8,128)(2,1)})) %all-reduce.17.cloned.1.call-update) | async-done | bytes 147472 | tf_op jit(solution)/shard_map/psum | solution.py:196
  963.8 20.3 %all-reduce.15.cloned.1.call-done = (bf16[1000,24]{0,1:T(8,128)(2,1)}, bf16[384,72]{0,1:T(8,128)(2,1)}, bf16[48]{0:T(256)(128)(2,1)}, bf16[384,24]{0,1:T(8,128)(...) async-done(((bf16[1000,24]{0,1:T(8,128)(2,1)}, bf16[384,72]{0,1:T(8,128)(2,1)}, bf16[48]{0:T(256)(128)(2,1)}, ...) | async-done | bytes 122176 | tf_op jit(solution)/shard_map/psum | solution.py:326
  994.1 122.4 %reduce-scatter.24.cloned.1.call-done = f32[24,1152]{1,0:T(8,128)} async-done(((f32[384,1152]{1,0:T(8,128)}), f32[24,1152]{1,0:T(8,128)}) %reduce-scatter.24.cloned.1.call-update) | async-done | bytes 110608
  (423 shorter events, 226.5 us)
Async XLA Ops:
  7.2 118.4 %copy-start = (bf16[384,1536]{1,0:T(8,128)(2,1)S(1)}, bf16[384,1536]{1,0:T(8,128)(2,1)}, u32[]{:S(2)}) copy-start(bf16[384,1536]{1,0:T(8,128)(2,1)} %param.43) | copy-start | bytes 3538948
  7.2 88.5 %all-gather.5.cloned.1.call-start = ((), (), s32[]{:S(2)}) async-start(), calls=%async_computation.7 | async-start | bytes 2359296 | tf_op jit(solution)/shard_map/all_gather | solution.py:108
  8.0 52.9 %copy-start.6 = (bf16[4,256,384]{2,1,0:T(8,128)(2,1)S(1)}, bf16[4,256,384]{2,1,0:T(8,128)(2,1)}, u32[]{:S(2)}) copy-start(bf16[4,256,384]{2,1,0:T(8,128)(2,1)} %param.27) | copy-start | bytes 2359300
  61.2 7.4 copy-start.37
  62.3 28.9 %copy-start.39 = (s32[4,256]{1,0:T(4,128)}, s32[4,256]{1,0:T(4,128)S(1)}, u32[]{:S(2)}) copy-start(s32[4,256]{1,0:T(4,128)S(1)} %constant_dynamic-slice_fusion.10) | copy-start | bytes 12292
  76.3 19.5 %all-gather.7.cloned.1.call-start = ((), (), s32[]{:S(2)}) async-start(), calls=%async_computation.8 | async-start | bytes 2359296 | tf_op jit(solution)/shard_map/all_gather | solution.py:107
  79.0 105.5 %all-gather.11.cloned.1.call-start = ((), (), s32[]{:S(2)}) async-start(), calls=%async_computation.10 | async-start | bytes 2359296 | tf_op jit(solution)/shard_map/all_gather | solution.py:237
  90.0 56.9 %copy-start.47 = (f32[4,256]{1,0:T(4,128)}, f32[4,256]{1,0:T(4,128)S(1)}, u32[]{:S(2)}) copy-start(f32[4,256]{1,0:T(4,128)S(1)} %dynamic-slice_convert_fusion) | copy-start | bytes 12292
  121.7 23.1 %copy-start.2 = (f32[4,256,384]{2,1,0:T(8,128)}, f32[4,256,384]{2,1,0:T(8,128)S(1)}, u32[]{:S(2)}) copy-start(f32[4,256,384]{2,1,0:T(8,128)S(1)} %get-tuple-element.312) | copy-start | bytes 4718596
  121.7 23.0 %copy-start.35 = (f32[4,256]{1,0:T(4,128)}, f32[4,256]{1,0:T(4,128)S(1)}, u32[]{:S(2)}) copy-start(f32[4,256]{1,0:T(4,128)S(1)} %broadcast_multiply_fusion.1) | copy-start | bytes 12292
  122.1 22.6 %copy-start.41 = (f32[4,256]{1,0:T(4,128)}, f32[4,256]{1,0:T(4,128)S(1)}, u32[]{:S(2)}) copy-start(f32[4,256]{1,0:T(4,128)S(1)} %fusion.99) | copy-start | bytes 12292
  153.4 34.1 %all-gather.9.cloned.1.call-start = ((), (), s32[]{:S(2)}) async-start(), calls=%async_computation.9 | async-start | bytes 2359296 | tf_op jit(solution)/shard_map/all_gather | solution.py:236
  153.9 140.3 %reduce-scatter.22.cloned.1.call-start = ((), (), s32[]{:S(2)}) async-start(), calls=%async_computation.14 | async-start | bytes 884736
  279.7 136.7 %reduce-scatter.28.cloned.1.call-start = ((), (), s32[]{:S(2)}) async-start(), calls=%async_computation.17 | async-start | bytes 626688
  282.4 266.5 %reduce-scatter.20.cloned.1.call-start = ((), (), s32[]{:S(2)}) async-start(), calls=%async_computation.13 | async-start | bytes 2506752 | tf_op jit(solution)/shard_map/reduce_scatter | solution.py:191
  287.9 394.2 %reduce-scatter.18.cloned.1.call-start = ((), (), s32[]{:S(2)}) async-start(), calls=%async_computation.12 | async-start | bytes 2506752 | tf_op jit(solution)/shard_map/reduce_scatter | solution.py:189
  294.2 516.6 %reduce-scatter.16.cloned.1.call-start = ((), (), s32[]{:S(2)}) async-start(), calls=%async_computation.11 | async-start | bytes 1671168 | tf_op jit(solution)/shard_map/reduce_scatter | solution.py:319
  300.1 640.6 %reduce-scatter.26.cloned.1.call-start = ((), (), s32[]{:S(2)}) async-start(), calls=%async_computation.16 | async-start | bytes 1880064
  304.5 656.2 %all-reduce.17.cloned.1.call-start = ((), (), s32[]{:S(2)}) async-start(), calls=%async_computation.19 | async-start | bytes 294912 | tf_op jit(solution)/shard_map/psum | solution.py:196
  307.0 376.8 %copy-start.57 = (f32[384]{0:T(512)S(1)}, f32[384]{0:T(512)}, u32[]{:S(2)}) copy-start(f32[384]{0:T(512)} %get-tuple-element.309) | copy-start | bytes 4612
  307.0 376.8 %copy-start.59 = (f32[1536]{0:T(1024)S(1)}, f32[1536]{0:T(1024)}, u32[]{:S(2)}) copy-start(f32[1536]{0:T(1024)} %get-tuple-element.345) | copy-start | bytes 18436
  683.7 300.4 %all-reduce.15.cloned.1.call-start = ((), (), s32[]{:S(2)}) async-start(), calls=%async_computation.18 | async-start | bytes 250880 | tf_op jit(solution)/shard_map/psum | solution.py:326
  942.3 174.2 %reduce-scatter.24.cloned.1.call-start = ((), (), s32[]{:S(2)}) async-start(), calls=%async_computation.15 | async-start | bytes 1880064
  942.3 174.2 %copy-start.1 = (bf16[384,1536]{1,0:T(8,128)(2,1)S(1)}, bf16[384,1536]{1,0:T(8,128)(2,1)}, u32[]{:S(2)}) copy-start(bf16[384,1536]{1,0:T(8,128)(2,1)} %param.43) | copy-start | bytes 3538948
  (69 other events, 204.7 us)
Sparse Core Ops, SparseCore 0:
  76.4 5.5 all-gather.4
  83.5 10.8 all-gather.6
  153.5 9.5 all-gather.10
  164.4 10.8 all-gather.8
  279.8 7.9 reduce-scatter.21
  293.0 123.3 reduce-scatter.27
  421.4 127.5 reduce-scatter.19
  554.6 127.4 reduce-scatter.17
  686.9 123.7 reduce-scatter.15
  815.4 125.2 reduce-scatter.25
  943.7 16.9 all-reduce.16
  964.5 19.5 all-reduce.14
  989.6 126.8 reduce-scatter.23
where the time goes:
time: 1130 us; the launch traced here: 1120 us
  waiting for transfers between devices  706 us (62%)
  blocking collectives  129 us (11%)
  matrix products  112 us (10%)
  local copies, waits for them, and re-layouts  92.8 us (8%)
  other arithmetic  64.4 us (6%)
  between operations  17.4 us (2%)
    unnamed x17, waiting for transfers between devices  360 us
    reduce_scatter x1, waiting for transfers between devices, body(): lax.psum_scatter(grad_w_fc1, 'bucket', scatter_dimension=1, tiled=True)  132 us
    reduce_scatter x1, waiting for transfers between devices, body(): lax.psum_scatter(grad_w_fc2, 'bucket', scatter_dimension=0, tiled=True)  129 us
    unnamed x1, blocking collectives  75.1 us
    reduce_scatter x1, waiting for transfers between devices, body(): lax.psum_scatter(grad_table, 'bucket', scatter_dimension=1, tiled=True)  48.7 us
    all_gather x1, blocking collectives, body(): ada_full = lax.all_gather(w_ada, 'bucket', axis=0, tiled=True)  48 us
    unnamed x161, local copies, waits for them, and re-layouts  27.3 us
    dynamic_slice x24, local copies, waits for them, and re-layouts, body(): lax.map(attend, (query, key_rows, value_rows, same_crop))  24.4 us
  transfers between devices with their start and end apart: 13, of which 8 were waited for; matrix products, arithmetic and copies ran while one was open for 9% of the time, Pallas kernels for 0%

commit v1 on v0

v1 whole, which is shorter than its diff:
```python
from functools import partial
import math

import jax
import jax.numpy as jnp
from jax import lax
from jax.experimental import pallas as pl
from jax.experimental.pallas import tpu as pltpu
from jax.sharding import PartitionSpec as P

D = 384
HEADS = 6
HEAD_DIM = 64
FF = 1536
NCLASS = 1000
CGROUPS = 24
CROPS = 8
EPSILON = 1e-06
NEGATIVE = -1e30
PAIR = 2 * HEAD_DIM
TOK = 256
FCH = 256
GELU_A = math.sqrt(2.0 / math.pi)
GELU_B = 0.044715
F32 = jnp.float32
BF16 = jnp.bfloat16


def dot(left, right):
    return jnp.dot(left, right, preferred_element_type=F32)


def dot_nt(left, right):
    return lax.dot_general(left, right, (((1,), (1,)), ((), ())), preferred_element_type=F32)


def dot_tn(left, right):
    return lax.dot_general(left, right, (((0,), (0,)), ((), ())), preferred_element_type=F32)


def normalise(values):
    centred = values - jnp.mean(values, -1, keepdims=True)
    inverse = lax.rsqrt(jnp.mean(centred * centred, -1, keepdims=True) + EPSILON)
    return centred * inverse, inverse


def normalise_back(grad, normal, inverse):
    return inverse * (
        grad
        - jnp.mean(grad, -1, keepdims=True)
        - normal * jnp.mean(grad * normal, -1, keepdims=True)
    )


def three_terms(values):
    high = values.astype(BF16).astype(F32)
    rest = values - high
    middle = rest.astype(BF16).astype(F32)
    last = rest - middle
    return jnp.concatenate([high, middle, last, jnp.zeros_like(last)], 0).astype(BF16)


def crop_rows(column, count):
    lane = lax.broadcasted_iota(jnp.int32, (count, 4 * CROPS), 1)
    return jnp.where((lane & (CROPS - 1)).astype(F32) == column, 1.0, 0.0).astype(BF16)


def crop_columns(row, count):
    line = lax.broadcasted_iota(jnp.int32, (2 * CROPS, count), 0).astype(F32)
    return jnp.where(line == row, 1.0, 0.0).astype(BF16)


def half_lanes(values, half):
    lane = lax.broadcasted_iota(jnp.int32, values.shape, 1)
    return jnp.where((lane // HEAD_DIM) == half, values, jnp.zeros_like(values))


def forward_kernel(
    place,
    tok_own,
    tok_in,
    cot_own,
    cot_in,
    col,
    row,
    mod,
    head_tab,
    chan_tab,
    w_qkv,
    b_qv,
    w_proj,
    b_proj,
    w_fc1,
    b_fc1,
    w_fc2,
    b_fc2,
    w_router,
    out_own,
    out_far,
    hid_out,
    q_out,
    k_out,
    v_out,
    prob_out,
    gheads_out,
    gres_out,
    dw1,
    dw2,
    dwp,
    db1,
    db2,
    dbp,
    dwr,
    gmod,
    x_s,
    cot_s,
    bias_s,
    hot_s,
    tab_s,
    mix_s,
    att_s,
    branch_s,
    res_s,
    h2_s,
    coef_s,
    gml_s,
    mlp_s,
    gh2_s,
    gm_s,
):
    length = x_s.shape[0]
    local = tok_own.shape[1]
    far = tok_in.shape[0]

    @pl.when(pl.program_id(0) == 0)
    def _():
        for ref in (dw1, dw2, dwp, db1, db2, dbp, dwr):
            ref[...] = jnp.zeros_like(ref)

    x_s[0:local] = tok_own[0].astype(F32)
    cot_s[0:local] = cot_own[0].astype(F32)
    for j in range(far):
        x_s[(j + 1) * local : (j + 2) * local] = tok_in[j, 0].astype(F32)
        cot_s[(j + 1) * local : (j + 2) * local] = cot_in[j, 0].astype(F32)
    tab_s[...] = three_terms(mod[0])
    mlp_s[...] = jnp.zeros_like(mlp_s)
    gh2_s[...] = jnp.zeros_like(gh2_s)
    gm_s[...] = jnp.zeros_like(gm_s)
    id_row = row[0, 0:1, :]

    def first(i, _):
        part = pl.ds(i * TOK, TOK)
        hot = crop_rows(col[0, part, 0:1], TOK)
        hot_s[part] = hot
        bias_s[part] = jnp.where(col[0, part, 1:2] == id_row, 0.0, NEGATIVE)
        normal, _ = normalise(x_s[part])
        hidden = (normal * (1.0 + dot(hot, tab_s[:, D : 2 * D])) + dot(hot, tab_s[:, 0:D])).astype(
            BF16
        )
        hid_out[0, part] = hidden
        q_out[0, part] = (dot(hidden, w_qkv[:, 0:D]) + b_qv[:, 0:D]).astype(BF16) * BF16(
            HEAD_DIM**-0.5
        )
        k_out[0, part] = dot(hidden, w_qkv[:, D : 2 * D]).astype(BF16)
        v_out[0, part] = (dot(hidden, w_qkv[:, 2 * D :]) + b_qv[:, D:]).astype(BF16)
        return 0

    lax.fori_loop(0, length // TOK, first, 0)

    def attend(hp, _):
        lanes = pl.ds(pl.multiple_of(hp * PAIR, PAIR), PAIR)
        query, key = q_out[0, :, lanes], k_out[0, :, lanes]
        value_t = v_out[0, :, lanes].T
        for half in range(2):
            key_half = half_lanes(key, half)
            for c in range(length // TOK):
                cols = slice(c * TOK, (c + 1) * TOK)
                scores = dot_nt(key_half, query[cols]) + bias_s[:, cols]
                top = jnp.max(scores, 0, keepdims=True)
                numerator = jnp.exp(scores - top)
                scale = 1.0 / jnp.sum(numerator, 0, keepdims=True)
                prob = (numerator * scale).astype(BF16)
                prob_out[0, 2 * hp + half, :, cols] = prob
                mix_s[half * HEAD_DIM : (half + 1) * HEAD_DIM, cols] = dot(
                    value_t[half * HEAD_DIM : (half + 1) * HEAD_DIM], prob
                )
        keep_heads = dot(hot_s[...], head_tab[0, :, lanes])
        att_s[:, lanes] = (mix_s[...].T * keep_heads).astype(BF16)
        return 0

    lax.fori_loop(0, D // PAIR, attend, 0)

    def middle(i, _):
        part = pl.ds(i * TOK, TOK)
        hot = hot_s[part]
        live = jnp.where(col[0, part, 1:2] >= 0.0, 1.0, 0.0)
        branch = dot(att_s[part], w_proj[...]) + b_proj[...]
        branch_s[part] = branch
        residual = x_s[part] + live * dot(hot, tab_s[:, 2 * D : 3 * D]) * branch
        res_s[part] = residual
        normal, _ = normalise(residual)
        hidden = (
            normal * (1.0 + dot(hot, tab_s[:, 4 * D : 5 * D])) + dot(hot, tab_s[:, 3 * D : 4 * D])
        ).astype(BF16)
        h2_s[part] = hidden
        logit = jnp.sum(hidden.astype(F32) * w_router[...], -1, keepdims=True)
        rate = 1.0 / (1.0 + jnp.exp(-logit))
        keep = live * col[0, part, 2:3]
        coef = keep * rate
        coef_s[part, 0:1] = coef
        coef_s[part, 1:2] = coef * (1.0 - rate)
        gml = (cot_s[part] * coef * dot(hot, tab_s[:, 5 * D : 6 * D])).astype(BF16)
        gml_s[part] = gml
        db2[...] += jnp.sum(gml.astype(F32), 0, keepdims=True)
        return 0

    lax.fori_loop(0, length // TOK, middle, 0)

    def feed(c, _):
        units = pl.ds(pl.multiple_of(c * FCH, FCH), FCH)
        hidden, gml = h2_s[...], gml_s[...]
        pre = dot(hidden, w_fc1[:, units]) + b_fc1[:, units]
        mask = dot(hot_s[...], chan_tab[0, :, units])
        square = pre * pre
        tanh = jnp.tanh(pre * (GELU_A + (GELU_A * GELU_B) * square))
        half = 0.5 * pre
        side = 0.5 + 0.5 * tanh
        act = (pre * side * mask).astype(BF16)
        slope = side + half * (1.0 - tanh * tanh) * (GELU_A + (3.0 * GELU_A * GELU_B) * square)
        mlp_s[...] += dot(act, w_fc2[units, :])
        dw2[units, :] += dot_tn(act, gml)
        gpre = (slope * mask * dot_nt(gml, w_fc2[units, :])).astype(BF16)
        dw1[units, :] += dot_tn(gpre, hidden)
        db1[:, units] += jnp.sum(gpre.astype(F32), 0, keepdims=True)
        gh2_s[...] += dot_nt(gpre, w_fc1[:, units])
        return 0

    lax.fori_loop(0, FF // FCH, feed, 0)

    def last(i, _):
        part = pl.ds(i * TOK, TOK)
        hot = hot_s[part]
        live = jnp.where(col[0, part, 1:2] >= 0.0, 1.0, 0.0)
        coef = coef_s[part, 0:1]
        cot = cot_s[part]
        mlp = mlp_s[part] + b_fc2[...]
        gate2 = dot(hot, tab_s[:, 5 * D : 6 * D])
        residual = res_s[part]
        outcome = (residual + coef * gate2 * mlp).astype(BF16)
        mlp_s[part] = outcome.astype(F32)
        cot_mlp = cot * mlp
        grad_logit = jnp.sum(cot_mlp * gate2, -1, keepdims=True) * coef_s[part, 1:2]
        hidden = h2_s[part].astype(F32)
        dwr[...] += jnp.sum(hidden * grad_logit, 0, keepdims=True)
        grad_hidden = gh2_s[part] + grad_logit * w_router[...]
        normal, inverse = normalise(residual)
        grad_res = cot + normalise_back(
            grad_hidden * (1.0 + dot(hot, tab_s[:, 4 * D : 5 * D])), normal, inverse
        )
        gres_out[0, part] = grad_res
        grad_live = grad_res * live
        grad_branch = (grad_live * dot(hot, tab_s[:, 2 * D : 3 * D])).astype(BF16)
        hot_t = crop_columns(row[0, 1:2, part], TOK)
        gm_s[:, 0:D] += dot(hot_t, (grad_live * branch_s[part]).astype(BF16))
        gm_s[:, D : 2 * D] += dot(hot_t, grad_hidden.astype(BF16))
        gm_s[:, 2 * D : 3 * D] += dot(hot_t, (grad_hidden * normal).astype(BF16))
        gm_s[:, 3 * D : 4 * D] += dot(hot_t, (cot_mlp * coef).astype(BF16))
        dbp[...] += jnp.sum(grad_branch.astype(F32), 0, keepdims=True)
        dwp[...] += dot_tn(grad_branch, att_s[part])
        gheads_out[0, part] = (
            dot_nt(grad_branch, w_proj[...]).astype(BF16).astype(F32) * dot(hot, head_tab[0])
        ).astype(BF16)
        return 0

    lax.fori_loop(0, length // TOK, last, 0)
    out_own[0] = mlp_s[0:local].astype(BF16)
    for j in range(far):
        out_far[j, 0] = mlp_s[(j + 1) * local : (j + 2) * local].astype(BF16)
    gmod[0] = gm_s[0:CROPS]


def backward_kernel(
    place,
    tok_own,
    tok_in,
    col,
    row,
    mod,
    w_qkv,
    hid,
    q_in,
    k_in,
    v_in,
    prob_in,
    gheads,
    gres,
    gt_own,
    gt_far,
    dwq,
    dbq,
    gmod,
    gp_s,
    dk_s,
    dv_s,
    dq_s,
    x_s,
    tab_s,
    gm_s,
):
    length = x_s.shape[0]
    local = tok_own.shape[1]
    far = tok_in.shape[0]

    @pl.when(pl.program_id(0) == 0)
    def _():
        for ref in (dwq, dbq):
            ref[...] = jnp.zeros_like(ref)

    x_s[0:local] = tok_own[0].astype(F32)
    for j in range(far):
        x_s[(j + 1) * local : (j + 2) * local] = tok_in[j, 0].astype(F32)
    tab_s[...] = three_terms(mod[0, :, D : 2 * D])
    gm_s[...] = jnp.zeros_like(gm_s)

    def attend(hp, _):
        lanes = pl.ds(pl.multiple_of(hp * PAIR, PAIR), PAIR)
        query, key, value = q_in[0, :, lanes], k_in[0, :, lanes], v_in[0, :, lanes]
        grad = gheads[0, :, lanes]
        key_t = key.T
        dk_s[...] = jnp.zeros_like(dk_s)
        dv_s[...] = jnp.zeros_like(dv_s)
        for half in range(2):
            value_half = half_lanes(value, half)
            for c in range(length // TOK):
                cols = slice(c * TOK, (c + 1) * TOK)
                prob_low = prob_in[0, 2 * hp + half, :, cols]
                prob = prob_low.astype(F32)
                grad_cols = grad[cols]
                product = prob * dot_nt(value_half, grad_cols)
                inner = jnp.sum(product, 0, keepdims=True)
                grad_scores = (product - prob * inner).astype(BF16)
                dv_s[...] += dot(prob_low, half_lanes(grad_cols, half))
                dk_s[...] += dot(grad_scores, half_lanes(query[cols], half))
                dq_s[half * HEAD_DIM : (half + 1) * HEAD_DIM, cols] = dot(
                    key_t[half * HEAD_DIM : (half + 1) * HEAD_DIM], grad_scores
                )
        gp_s[:, lanes] = (dq_s[...].T * HEAD_DIM**-0.5).astype(BF16)
        gp_s[:, pl.ds(pl.multiple_of(D + hp * PAIR, PAIR), PAIR)] = dk_s[...].astype(BF16)
        gp_s[:, pl.ds(pl.multiple_of(2 * D + hp * PAIR, PAIR), PAIR)] = dv_s[...].astype(BF16)
        return 0

    lax.fori_loop(0, D // PAIR, attend, 0)

    def last(i, _):
        part = pl.ds(i * TOK, TOK)
        hot = crop_rows(col[0, part, 0:1], TOK)
        grad = gp_s[part]
        dbq[...] += jnp.sum(grad.astype(F32), 0, keepdims=True)
        grad_hidden = dot_nt(grad, w_qkv[...])
        normal, inverse = normalise(x_s[part])
        hot_t = crop_columns(row[0, 1:2, part], TOK)
        gm_s[:, 0:D] += dot(hot_t, grad_hidden.astype(BF16))
        gm_s[:, D : 2 * D] += dot(hot_t, (grad_hidden * normal).astype(BF16))
        x_s[part] = gres[0, part] + normalise_back(
            grad_hidden * (1.0 + dot(hot, tab_s[...])), normal, inverse
        )
        return 0

    lax.fori_loop(0, length // TOK, last, 0)
    for c in range(3):
        rows = slice(c * D, (c + 1) * D)
        dwq[rows, :] += dot_tn(gp_s[:, rows], hid[0])
    gt_own[0] = x_s[0:local].astype(BF16)
    for j in range(far):
        gt_far[j, 0] = x_s[(j + 1) * local : (j + 2) * local].astype(BF16)
    gmod[0] = gm_s[0:CROPS]


def whole(shape):
    return pl.BlockSpec(shape, lambda r, place: (0,) * len(shape))


def per_row(shape):
    return pl.BlockSpec((1,) + shape, lambda r, place: (r,) + (0,) * len(shape))


def per_far(count, shape):
    return pl.BlockSpec((count, 1) + shape, lambda r, place: (0, r) + (0,) * len(shape))


def body(
    tokens,
    cotangent,
    segment_ids,
    pad_counts,
    timesteps,
    classes,
    head_mask,
    channel_mask,
    keep_mask,
    class_table,
    w_ada,
    b_ada,
    w_qkv,
    bias_qv,
    w_proj,
    b_proj,
    w_fc1,
    b_fc1,
    w_fc2,
    b_fc2,
    w_router,
):
    seqs, buckets = lax.axis_size("seq"), lax.axis_size("bucket")
    me_s, me_b = lax.axis_index("seq"), lax.axis_index("bucket")
    row_count, local, _ = tokens.shape
    mine = row_count // seqs
    length = local * seqs
    crops_here = row_count * CROPS
    crops_mine = mine * CROPS
    inner, outer = 4, buckets // 4

    def seq_hop(value, step):
        return lax.ppermute(value, "seq", [(i, i ^ step) for i in range(seqs)])

    def plane_hop(value, step):
        return lax.ppermute(value, "bucket", [(i, i ^ step) for i in range(buckets)])

    def line_hop(value, step):
        return lax.ppermute(value, "bucket", [(i, i ^ (step * inner)) for i in range(buckets)])

    def slab(value, device, count):
        return lax.dynamic_slice_in_dim(value, device * count, count, 0)

    def by_device(pieces, device):
        chosen = pieces[0]
        for j in range(1, seqs):
            chosen = jnp.where((me_s ^ device) == j, pieces[j], chosen)
        return chosen

    def deal_rows(value):
        return [seq_hop(slab(value, me_s ^ j, mine), j) for j in range(1, seqs)]

    tok_in = jnp.stack(deal_rows(tokens))
    cot_in = jnp.stack(deal_rows(cotangent))
    keep_in = deal_rows(keep_mask)

    ada_parts = [w_ada] + [line_hop(w_ada, k) for k in range(1, outer)]
    ada_line = jnp.concatenate(ada_parts, 0)
    ada_all = jnp.concatenate([ada_line] + [plane_hop(ada_line, k) for k in range(1, inner)], 0)

    position = jnp.arange(length, dtype=jnp.int32)
    live_row = position[None, :] < (length - pad_counts)[:, None]
    attend_ids = jnp.where(live_row, segment_ids, -1)
    both = jnp.stack([segment_ids, attend_ids]).astype(F32)
    both = lax.dynamic_slice_in_dim(both, me_s * mine, mine, 1)
    both = jnp.concatenate(
        [lax.dynamic_slice_in_dim(both, (me_s ^ j) * local, local, 2) for j in range(seqs)], 2
    )
    keep_all = jnp.concatenate([slab(keep_mask, me_s, mine)] + keep_in, 1).astype(F32)
    col = jnp.stack([both[0], both[1], keep_all, keep_all], -1)
    row = jnp.stack([both[1], both[0]], 1)

    half_width = D // 2
    frequency = jnp.exp(-math.log(10000.0) * jnp.arange(half_width, dtype=F32) / half_width)
    angles = timesteps.reshape(crops_here, 1).astype(F32) * frequency
    class_ids = classes.reshape(crops_here)
    class_hot = (class_ids[:, None] == jnp.arange(NCLASS, dtype=jnp.int32)).astype(BF16)
    condition = jnp.concatenate([jnp.cos(angles), jnp.sin(angles)], -1) + dot(
        class_hot, class_table
    )
    sigmoid = 1.0 / (1.0 + jnp.exp(-condition))
    silu_low = (condition * sigmoid).astype(BF16)
    silu_slope = sigmoid * (1.0 + condition * (1.0 - sigmoid))
    near = jnp.arange(buckets)
    order = me_b ^ ((near // outer) + inner * (near % outer))
    depth = D // buckets
    silu_near = jnp.take(silu_low.reshape(crops_here, buckets, depth), order, axis=1).reshape(
        crops_here, D
    )
    slope_near = jnp.take(silu_slope.reshape(crops_here, buckets, depth), order, axis=1).reshape(
        crops_here, D
    )
    mod_part = dot(silu_near, ada_all) + b_ada.astype(F32)
    mod_pieces = [slab(mod_part, me_s, crops_mine)] + deal_rows_of(mod_part, seqs, me_s, crops_mine)
    modulation = jnp.concatenate([by_device(mod_pieces, d) for d in range(seqs)], 1).reshape(
        mine, CROPS, 6 * D
    )

    def table_of(mask, width):
        wide = jnp.repeat(mask, width, axis=-1).astype(BF16)
        return jnp.pad(wide, ((0, 0), (0, 3 * CROPS), (0, 0)))

    head_tab = table_of(slab(head_mask, me_s, mine), HEAD_DIM)
    chan_tab = table_of(slab(channel_mask, me_s, mine), FF // CGROUPS)
    place = me_s.reshape(1).astype(jnp.int32)
    own = pl.BlockSpec((1, local, D), lambda r, place: (place[0] * mine + r, 0, 0))
    far = seqs - 1
    bias_row = bias_qv.astype(F32).reshape(1, 2 * D)

    def struct(shape, kind=F32):
        return jax.ShapeDtypeStruct(shape, kind)

    fwd_shapes = [
        struct((mine, local, D), BF16),
        struct((far, mine, local, D), BF16),
        struct((mine, length, D), BF16),
        struct((mine, length, D), BF16),
        struct((mine, length, D), BF16),
        struct((mine, length, D), BF16),
        struct((mine, HEADS, length, length), BF16),
        struct((mine, length, D), BF16),
        struct((mine, length, D)),
        struct((FF, D)),
        struct((FF, D)),
        struct((D, D)),
        struct((1, FF)),
        struct((1, D)),
        struct((1, D)),
        struct((1, D)),
        struct((mine, CROPS, 4 * D)),
    ]
    fwd_out_specs = [
        per_row((local, D)),
        per_far(far, (local, D)),
        per_row((length, D)),
        per_row((length, D)),
        per_row((length, D)),
        per_row((length, D)),
        per_row((HEADS, length, length)),
        per_row((length, D)),
        per_row((length, D)),
        whole((FF, D)),
        whole((FF, D)),
        whole((D, D)),
        whole((1, FF)),
        whole((1, D)),
        whole((1, D)),
        whole((1, D)),
        per_row((CROPS, 4 * D)),
    ]
    tokens_here = mine * length
    (
        out_own,
        out_far,
        hid,
        query,
        key,
        value,
        prob,
        grad_heads,
        grad_res,
        dw1,
        dw2,
        dwp,
        db1,
        db2,
        dbp,
        dwr,
        gmod_late,
    ) = pl.pallas_call(
        forward_kernel,
        grid_spec=pltpu.PrefetchScalarGridSpec(
            num_scalar_prefetch=1,
            grid=(mine,),
            in_specs=[
                own,
                per_far(far, (local, D)),
                own,
                per_far(far, (local, D)),
                per_row((length, 4)),
                per_row((2, length)),
                per_row((CROPS, 6 * D)),
                per_row((4 * CROPS, D)),
                per_row((4 * CROPS, FF)),
                whole((D, 3 * D)),
                whole((1, 2 * D)),
                whole((D, D)),
                whole((1, D)),
                whole((D, FF)),
                whole((1, FF)),
                whole((FF, D)),
                whole((1, D)),
                whole((1, D)),
            ],
            out_specs=fwd_out_specs,
            scratch_shapes=[
                pltpu.VMEM((length, D), F32),
                pltpu.VMEM((length, D), F32),
                pltpu.VMEM((length, length), F32),
                pltpu.VMEM((length, 4 * CROPS), BF16),
                pltpu.VMEM((4 * CROPS, 6 * D), BF16),
                pltpu.VMEM((PAIR, length), F32),
                pltpu.VMEM((length, D), BF16),
                pltpu.VMEM((length, D), F32),
                pltpu.VMEM((length, D), F32),
                pltpu.VMEM((length, D), BF16),
                pltpu.VMEM((length, 2), F32),
                pltpu.VMEM((length, D), BF16),
                pltpu.VMEM((length, D), F32),
                pltpu.VMEM((length, D), F32),
                pltpu.VMEM((2 * CROPS, 4 * D), F32),
            ],
        ),
        out_shape=fwd_shapes,
        cost_estimate=pl.CostEstimate(
            flops=2 * tokens_here * (4 * D * D + 6 * D * FF + 2 * D * length),
            transcendentals=tokens_here * (FF + HEADS * length),
            bytes_accessed=20_000_000,
        ),
    )(
        place,
        tokens,
        tok_in,
        cotangent,
        cot_in,
        col,
        row,
        modulation,
        head_tab,
        chan_tab,
        w_qkv,
        bias_row,
        w_proj,
        b_proj.astype(F32).reshape(1, D),
        w_fc1,
        b_fc1.astype(F32).reshape(1, FF),
        w_fc2,
        b_fc2.astype(F32).reshape(1, D),
        w_router.astype(F32).reshape(1, D),
    )

    def return_rows(own_piece, far_pieces):
        pieces = [own_piece] + [seq_hop(far_pieces[j - 1], j) for j in range(1, seqs)]
        return jnp.concatenate([by_device(pieces, d) for d in range(seqs)], 0)

    def sum_over_all(parts):
        joined = jnp.concatenate([part.reshape(buckets, -1, D) for part in parts], 1)
        lines = joined.shape[1] // seqs
        joined = joined.reshape(buckets, seqs, lines, D)
        joined = jnp.take(joined, order, axis=0)
        total = lax.dynamic_index_in_dim(joined, me_s, 1, keepdims=False)
        for j in range(1, seqs):
            sent = lax.dynamic_index_in_dim(joined, me_s ^ j, 1, keepdims=False).astype(BF16)
            total = total + seq_hop(sent, j).astype(F32)
        total = sum_over_buckets(total)
        pieces = [total] + [seq_hop(total, j) for j in range(1, seqs)]
        return jnp.concatenate([by_device(pieces, d) for d in range(seqs)], 0)

    def sum_over_buckets(total):
        total = total.reshape((inner, outer) + total.shape[1:])
        plane = total[0]
        low = total.astype(BF16)
        for k in range(1, inner):
            plane = plane + plane_hop(low[k], k).astype(F32)
        line = plane[0]
        low = plane.astype(BF16)
        for k in range(1, outer):
            line = line + line_hop(low[k], k).astype(F32)
        return line

    output = return_rows(out_own, out_far)
    early = sum_over_all([dw1, dw2])

    gt_own, gt_far, dwq, dbq, gmod_first = pl.pallas_call(
        backward_kernel,
        grid_spec=pltpu.PrefetchScalarGridSpec(
            num_scalar_prefetch=1,
            grid=(mine,),
            in_specs=[
                own,
                per_far(far, (local, D)),
                per_row((length, 4)),
                per_row((2, length)),
                per_row((CROPS, 6 * D)),
                whole((D, 3 * D)),
                per_row((length, D)),
                per_row((length, D)),
                per_row((length, D)),
                per_row((length, D)),
                per_row((HEADS, length, length)),
                per_row((length, D)),
                per_row((length, D)),
            ],
            out_specs=[
                per_row((local, D)),
                per_far(far, (local, D)),
                whole((3 * D, D)),
                whole((1, 3 * D)),
                per_row((CROPS, 2 * D)),
            ],
            scratch_shapes=[
                pltpu.VMEM((length, 3 * D), BF16),
                pltpu.VMEM((length, PAIR), F32),
                pltpu.VMEM((length, PAIR), F32),
                pltpu.VMEM((PAIR, length), F32),
                pltpu.VMEM((length, D), F32),
                pltpu.VMEM((4 * CROPS, D), BF16),
                pltpu.VMEM((2 * CROPS, 2 * D), F32),
            ],
        ),
        out_shape=[
            struct((mine, local, D), BF16),
            struct((far, mine, local, D), BF16),
            struct((3 * D, D)),
            struct((1, 3 * D)),
            struct((mine, CROPS, 2 * D)),
        ],
        cost_estimate=pl.CostEstimate(
            flops=2 * tokens_here * (6 * D * D + 5 * D * length),
            transcendentals=0,
            bytes_accessed=20_000_000,
        ),
    )(
        place,
        tokens,
        tok_in,
        col,
        row,
        modulation,
        w_qkv,
        hid,
        query,
        key,
        value,
        prob,
        grad_heads,
        grad_res,
    )
    grad_tokens = return_rows(gt_own, gt_far)
    late = sum_over_all([dwq, dwp])

    grad_mod = jnp.concatenate([gmod_first, gmod_late], -1).astype(BF16).reshape(crops_mine, 6 * D)
    width = 6 * D // seqs
    mod_pieces = [lax.dynamic_slice_in_dim(grad_mod, me_s * width, width, 1)] + [
        seq_hop(lax.dynamic_slice_in_dim(grad_mod, (me_s ^ j) * width, width, 1), j)
        for j in range(1, seqs)
    ]
    grad_mod = jnp.concatenate([by_device(mod_pieces, d) for d in range(seqs)], 0)
    grad_w_ada = sum_over_buckets(
        lax.dot_general(
            silu_near, grad_mod, (((0,), (0,)), ((), ())), preferred_element_type=F32
        ).reshape(buckets, depth, width)
    )

    grad_b_ada = jnp.sum(grad_mod.astype(F32), 0).reshape(buckets, -1)
    grad_silu = dot_nt(grad_mod, ada_all)
    small = jnp.concatenate(
        [
            part.reshape(buckets, -1)
            for part in (
                db1,
                db2,
                dbp,
                dwr,
                jnp.concatenate([dbq[:, 0:D], dbq[:, 2 * D :]], 1),
            )
        ],
        1,
    )
    small_size = small.shape[1]
    for j in [1 << b for b in range(seqs.bit_length() - 1)]:
        grad_silu = grad_silu + seq_hop(grad_silu, j)
        small = small + seq_hop(small, j)
    grad_condition = grad_silu * slope_near
    crop_part = grad_condition.reshape(crops_here, buckets, depth).swapaxes(0, 1)
    parcel = jnp.concatenate(
        [
            crop_part.reshape(buckets, crops_here * depth),
            jnp.take(small, order, axis=0),
            jnp.take(grad_b_ada, order, axis=0),
            jnp.broadcast_to(class_ids.astype(F32)[None], (buckets, crops_here)),
        ],
        1,
    ).reshape(inner, outer, -1)
    parcel = jnp.stack([parcel[0]] + [plane_hop(parcel[k], k) for k in range(1, inner)])
    parcel = jnp.stack([parcel[:, 0]] + [line_hop(parcel[:, k], k) for k in range(1, outer)])
    parcel = parcel.reshape(buckets, -1)
    first = crops_here * depth
    crop_grads = parcel[:, :first].reshape(buckets * crops_here, depth)
    small = jnp.sum(parcel[:, first : first + small_size + grad_b_ada.shape[1]], 0)
    source_ids = parcel[:, first + small_size + grad_b_ada.shape[1] :].reshape(1, -1)
    hot = (jnp.arange(NCLASS, dtype=F32)[:, None] == source_ids).astype(F32)
    grad_table = jnp.dot(hot, crop_grads, precision=lax.Precision.HIGHEST)

    ff_part, d_part = FF // buckets, D // buckets
    cuts = [0]
    for size in (ff_part, d_part, d_part, d_part, 2 * d_part, grad_b_ada.shape[1]):
        cuts.append(cuts[-1] + size)
    v_b1, v_b2, v_bp, v_wr, v_qv, v_ada = (small[a:b] for a, b in zip(cuts[:-1], cuts[1:]))
    return (
        output,
        grad_tokens,
        grad_table,
        grad_w_ada,
        v_ada.reshape(1, -1),
        late[: 3 * d_part].T,
        v_qv,
        late[3 * d_part :].T,
        v_bp,
        early[:ff_part].T,
        v_b1,
        early[ff_part:],
        v_b2,
        v_wr,
    )


def deal_rows_of(value, seqs, me_s, count):
    return [
        lax.ppermute(
            lax.dynamic_slice_in_dim(value, (me_s ^ j) * count, count, 0),
            "seq",
            [(i, i ^ j) for i in range(seqs)],
        )
        for j in range(1, seqs)
    ]


def solution(mesh):
    placed = (
        P("bucket", "seq", None),
        P("bucket", "seq", None),
        P("bucket", None),
        P("bucket"),
        P("bucket", None),
        P("bucket", None),
        P("bucket", None, None),
        P("bucket", None, None),
        P("bucket", "seq"),
        P(),
        P("bucket", "seq"),
        P("seq"),
        P(),
        P(),
        P(),
        P(),
        P(),
        P(),
        P(),
        P(),
        P(),
    )
    return jax.shard_map(
        body,
        mesh=mesh,
        in_specs=placed,
        out_specs=(
            P("bucket", "seq", None),
            P("bucket", "seq", None),
            P(None, "bucket"),
            P("bucket", "seq"),
            P("seq", "bucket"),
            P(None, "bucket"),
            P("bucket"),
            P(None, "bucket"),
            P("bucket"),
            P(None, "bucket"),
            P("bucket"),
            P("bucket", None),
            P("bucket"),
            P("bucket"),
        ),
        check_vma=False,
    )
```

time: 1130 us -> 227 us (0.20)
  waiting for transfers between devices: 706 us -> 43 us
  blocking collectives: 129 us -> 0 us
  matrix products: 112 us -> 3.7 us
  Pallas kernels: 0 us -> 75.6 us
  local copies, waits for them, and re-layouts: 92.8 us -> 33.4 us
  starting transfers between devices: 1.25 us -> 41.6 us
  other arithmetic: 64.4 us -> 27.8 us
  between operations: 17.4 us -> 1.41 us
    unnamed x17 -> x0, waiting for transfers between devices: 360 us -> none
    reduce_scatter x3 -> x0, waiting for transfers between devices: 310 us -> none  [the longest x1 132 us: body(): lax.psum_scatter(grad_w_fc1, 'bucket', scatter_dimension=1, tiled=True)]
    dot_general x55 -> x5, matrix products: 112 us -> 3.7 us  [the longest x1 1.72 us: body(): grad_table = jnp.dot(hot, crop_grads, precision=lax.Precision.HIGHEST)]
    pallas_call x0 -> x2, Pallas kernels: none -> 75.6 us  [the longest x1 52.3 us: body(): pl.pallas_call(forward_kernel, grid_spec=pltpu.PrefetchScalarGridSpec(num...]
    unnamed x1 -> x0, blocking collectives: 75.1 us -> none
    all_gather x4 -> x0, blocking collectives: 53.9 us -> none  [the longest x1 48 us: body(): ada_full = lax.all_gather(w_ada, 'bucket', axis=0, tiled=True)]
    ppermute x0 -> x43, waiting for transfers between devices: none -> 43 us  [the longest x15 31.9 us: plane_hop(): lax.ppermute(value, 'bucket', [(i, i ^ step) for i in range(buckets)])]
    ppermute x0 -> x43, starting transfers between devices: none -> 41.6 us  [the longest x15 20.8 us: line_hop(): lax.ppermute(value, 'bucket', [(i, i ^ step * inner) for i in range(bucke...]
  transfers between devices with their start and end apart: 13 -> 43, of which waited for: 8 -> 22; matrix products, arithmetic and copies ran while one was open for 9% -> 24% of each run, Pallas kernels for 0% -> 10%
where the time goes in v1:
time: 227 us; the launch traced here: 226 us
  Pallas kernels  75.6 us (33%)
  waiting for transfers between devices  43 us (19%)
  starting transfers between devices  41.6 us (18%)
  local copies, waits for them, and re-layouts  33.4 us (15%)
  other arithmetic  27.8 us (12%)
  matrix products  3.7 us (2%)
    pallas_call x1, Pallas kernels, body(): pl.pallas_call(forward_kernel, grid_spec=pltpu.PrefetchScalarGridSpec(num...  52.3 us
    ppermute x15, waiting for transfers between devices, plane_hop(): lax.ppermute(value, 'bucket', [(i, i ^ step) for i in range(buckets)])  31.9 us
    pallas_call x1, Pallas kernels, body(): pl.pallas_call(backward_kernel, grid_spec=pltpu.PrefetchScalarGridSpec(nu...  23.3 us
    ppermute x15, starting transfers between devices, line_hop(): lax.ppermute(value, 'bucket', [(i, i ^ step * inner) for i in range(bucke...  20.8 us
    ppermute x15, starting transfers between devices, plane_hop(): lax.ppermute(value, 'bucket', [(i, i ^ step) for i in range(buckets)])  18.4 us
    ppermute x15, waiting for transfers between devices, line_hop(): lax.ppermute(value, 'bucket', [(i, i ^ step * inner) for i in range(bucke...  9.92 us
    gather x2, local copies, waits for them, and re-layouts, sum_over_all(): joined = jnp.take(joined, order, axis=0)  7.45 us
    unnamed x57, local copies, waits for them, and re-layouts  5.66 us
  transfers between devices with their start and end apart: 43, of which 22 were waited for; matrix products, arithmetic and copies ran while one was open for 24% of the time, Pallas kernels for 10%

profile of v1, /device:TPU:0, one launch (start us, length us, event | category | flops | bytes accessed | tf_op | source)
XLA Modules:
  0.0 226.5 jit_solution(8299264822546574360)
XLA Ops:
  0.7 4.1 %collective-permute-start.4 = (bf16[24,1152]{1,0:T(8,128)(2,1)}, bf16[24,1152]{1,0:T(8,128)(2,1)S(1)}, u32[]{:S(2)}, u32[]{:S(2)}) collective-permute-start(bf16[24,1152]{1,0:T(8,128)(2,1)} %param.31), channel_id=1, source_target_pairs={{0,16},{2,18},{4,20},{6,22},{8,24},{10,26},{12,28},{14,30},{16,0},... | collective-permute-start | bytes 165896 | tf_op jit(solution)/shard_map/ppermute | solution.py:430
  17.0 1.8 collective-permute-start.6
  27.3 11.4 %collective-permute-done.7 = bf16[96,1152]{1,0:T(8,128)(2,1)S(1)} collective-permute-done((bf16[96,1152]{1,0:T(8,128)(2,1)S(1)}, bf16[96,1152]{1,0:T(8,128)(2,1)S(1)}, u32[]{:S(2)}, u32[]{:S(2)}) %collective-permute-start.7) | collective-permute-done | bytes 221216 | tf_op jit(solution)/shard_map/ppermute | solution.py:427
  41.8 52.3 %shard_map.308 = (bf16[2,256,384]{2,1,0:T(8,128)(2,1)}, bf16[1,2,256,384]{3,2,1,0:T(8,128)(2,1)}, bf16[2,512,384]{2,1,0:T(8,128)(2,1)}, bf16[2,512,384]{2,1,0:T(...) custom-call(s32[1]{0:T(128)} %bitcast.place, ...), custom_call_target="tpu_custom_call" | custom-call | flops 9261023232 | bytes 20000000 | tf_op jit(solution)/shard_map/pallas_call | solution.py:561
  98.4 23.3 %shard_map.309 = (bf16[2,256,384]{2,1,0:T(8,128)(2,1)}, bf16[1,2,256,384]{3,2,1,0:T(8,128)(2,1)}, f32[1152,384]{1,0:T(8,128)}, f32[1,1152]{1,0:T(1,128)}, f32[2,8,768]{2,1,0:T(8,128)}) custom-call(s32[1]{0:T(128)} %bitcast.place, bf16[4,256,384]{2,1,0:T(8,128)(2,1)} %tok_own.3, bf16[1,2,256,384]{3,2,1,0:T(8,128)(2,1)} %bitcast.137, f32[2,512,4]{2,1,0:T(8,128)} %copy.44.col, ...), custom_call_target="tpu_custom_call" | custom-call | flops 3825205248 | bytes 20000000 | tf_op jit(solution)/shard_map/pallas_call | solution.py:665
  125.9 2.1 gather_fusion.4
  128.0 2.1 broadcast_select_fusion.1
  131.9 2.5 %pad_maximum_fusion = f32[16,192,384]{2,1,0:T(8,128)} fusion(f32[16,96,384]{2,1,0:T(8,128)S(1)} %bitcast.127, f32[16,96,384]{2,1,0:T(8,128)S(1)} %bitcast.126), kind=kLoop, calls=%fused_computation.6 | loop fusion | flops 1179648 | bytes 9437184 | tf_op jit(solution)/shard_map/concatenate | solution.py:638
  134.4 5.4 %gather_fusion.5 = f32[16,2,96,384]{3,2,1,0:T(8,128)} fusion(f32[16,2,96,384]{3,2,1,0:T(8,128)} %bitcast.122, s32[1024]{0:T(1024)S(1)} %pad_clamp_fusion), kind=kCustom, calls=%fused_computation.5 | custom fusion | bytes 9437248 | tf_op jit(solution)/shard_map/jit(_take)/gather | solution.py:641
  139.8 2.9 %broadcast_select_fusion = f32[16,2,96,384]{3,2,1,0:T(8,128)S(1)} fusion(f32[16,2,96,384]{3,2,1,0:T(8,128)} %gather_fusion.5, pred[16]{0:T(512)(128)(4,1)S(1)} %compare_and_fusion), kind=kLoop, calls=%fused_computation.10 | loop fusion | flops 1179648 | bytes 9437200 | tf_op jit(solution)/shard_map/jit(_take)/select_n | solution.py:641
  142.6 2.2 copy-done.2
  155.3 1.9 collective-permute-start.19
  157.3 2.0 collective-permute-start.20
  160.6 1.8 collective-permute-start.23
  167.9 2.0 collective-permute-done.23
  169.9 2.2 collective-permute-done.21
  178.7 2.3 %collective-permute-done.26 = bf16[24,1152]{1,0:T(8,128)(2,1)S(1)} collective-permute-done((bf16[24,1152]{1,0:T(8,128)(2,1)S(1)}, bf16[24,1152]{1,0:T(8,128)(2,1)S(1)}, u32[]{:S(2)}, u32[]{:S(2)}) %collective-permute-start.26) | collective-permute-done | bytes 55328 | tf_op jit(solution)/shard_map/ppermute | solution.py:430
  183.0 1.7 fusion.43
  191.5 2.3 %collective-permute-done.30 = bf16[4,48,384]{2,1,0:T(8,128)(2,1)S(1)} collective-permute-done((bf16[4,48,384]{2,1,0:T(8,128)(2,1)S(1)}, bf16[4,48,384]{2,1,0:T(8,128)(2,1)S(1)}, u32[]{:S(2)}, u32[]{:S(2)}) %collective-permute-start.30) | collective-permute-done | bytes 147488 | tf_op jit(solution)/shard_map/ppermute | solution.py:427
  197.1 1.7 collective-permute-start.32
  204.1 5.4 %collective-permute-done.36 = bf16[4,96,384]{2,1,0:T(8,128)(2,1)S(1)} collective-permute-done((bf16[4,96,384]{2,1,0:T(8,128)(2,1)S(1)}, bf16[4,96,384]{2,1,0:T(8,128)(2,1)S(1)}, u32[]{:S(2)}, u32[]{:S(2)}) %collective-permute-start.36) | collective-permute-done | bytes 294944 | tf_op jit(solution)/shard_map/ppermute | solution.py:427
  209.4 3.7 %collective-permute-done.38 = bf16[4,96,384]{2,1,0:T(8,128)(2,1)S(1)} collective-permute-done((bf16[4,96,384]{2,1,0:T(8,128)(2,1)S(1)}, bf16[4,96,384]{2,1,0:T(8,128)(2,1)S(1)}, u32[]{:S(2)}, u32[]{:S(2)}) %collective-permute-start.38) | collective-permute-done | bytes 294944 | tf_op jit(solution)/shard_map/ppermute | solution.py:427
  214.7 1.8 collective-permute-start.39
  219.6 3.2 %collective-permute-done.41 = bf16[96,384]{1,0:T(8,128)(2,1)S(1)} collective-permute-done((bf16[96,384]{1,0:T(8,128)(2,1)S(1)}, bf16[96,384]{1,0:T(8,128)(2,1)S(1)}, u32[]{:S(2)}, u32[]{:S(2)}) %collective-permute-start.41) | collective-permute-done | bytes 73760 | tf_op jit(solution)/shard_map/ppermute | solution.py:430
  (253 shorter events, 83.0 us)
Async XLA Ops:
  0.7 16.2 %collective-permute-start.4 = (bf16[24,1152]{1,0:T(8,128)(2,1)}, bf16[24,1152]{1,0:T(8,128)(2,1)S(1)}, u32[]{:S(2)}, u32[]{:S(2)}) collective-permute-start(bf16[24,1152]{1,0:T(8,128)(2,1)} %param.31), channel_id=1, source_target_pairs={{0,16},{2,18},{4,20},{6,22},{8,24},{10,26},{12,28},{14,30},{16,0},... | collective-permute-start | bytes 165896 | tf_op jit(solution)/shard_map/ppermute | solution.py:430
  4.8 12.1 %collective-permute-start.3 = (bf16[24,1152]{1,0:T(8,128)(2,1)}, bf16[24,1152]{1,0:T(8,128)(2,1)S(1)}, u32[]{:S(2)}, u32[]{:S(2)}) collective-permute-start(bf16[24,1152]{1,0:T(8,128)(2,1)} %param.31), channel_id=1, source_target_pairs={{0,8},{2,10},{4,12},{6,14},{8,0},{10,2},{12,4},{14,6},{16,24},{18,... | collective-permute-start | bytes 165896 | tf_op jit(solution)/shard_map/ppermute | solution.py:430
  6.4 10.6 %collective-permute-start.5 = (bf16[24,1152]{1,0:T(8,128)(2,1)}, bf16[24,1152]{1,0:T(8,128)(2,1)S(1)}, u32[]{:S(2)}, u32[]{:S(2)}) collective-permute-start(bf16[24,1152]{1,0:T(8,128)(2,1)} %param.31), channel_id=1, source_target_pairs={{0,24},{2,26},{4,28},{6,30},{8,16},{10,18},{12,20},{14,22},{16,8},... | collective-permute-start | bytes 165896 | tf_op jit(solution)/shard_map/ppermute | solution.py:430
  7.2 18.2 %collective-permute-start.2 = (s32[2,256]{1,0:T(2,128)S(1)}, s32[2,256]{1,0:T(2,128)S(1)}, u32[]{:S(2)}, u32[]{:S(2)}) collective-permute-start(s32[2,256]{1,0:T(2,128)S(1)} %get-tuple-element.123), channel_id=1, source_target_pairs={{0,1},{1,0},{2,3},{3,2},{4,5},{5,4},{6,7},{7,6},{8,9},{9,8},{10,11... | collective-permute-start | bytes 6152 | tf_op jit(solution)/shard_map/ppermute | solution.py:424
  8.2 32.9 %collective-permute-start = (bf16[2,256,384]{2,1,0:T(8,128)(2,1)S(1)}, bf16[2,256,384]{2,1,0:T(8,128)(2,1)S(1)}, u32[]{:S(2)}, u32[]{:S(2)}) collective-permute-start(bf16[2,256,384]{2,1,0:T(8,128)(2,1)S(1)} %constant_dynamic-slice_fusion.6), channel_id=1, source_target_pairs={{0,1},{1,0},{2,3},{3,2},{4,5},{5,4},{6,7},{7,6},{8,9},{9,8},{10,11... | collective-permute-start | bytes 1179656 | tf_op jit(solution)/shard_map/ppermute | solution.py:424
  16.9 24.2 %collective-permute-start.1 = (bf16[2,256,384]{2,1,0:T(8,128)(2,1)S(1)}, bf16[2,256,384]{2,1,0:T(8,128)(2,1)}, u32[]{:S(2)}, u32[]{:S(2)}) collective-permute-start(bf16[2,256,384]{2,1,0:T(8,128)(2,1)S(1)} %constant_dynamic-slice_fusion.5), channel_id=1, source_target_pairs={{0,1},{1,0},{2,3},{3,2},{4,5},{5,4},{6,7},{7,6},{8,9},{9,8},{10,11... | collective-permute-start | bytes 1179656 | tf_op jit(solution)/shard_map/ppermute | solution.py:424
  17.0 10.3 %collective-permute-start.6 = (bf16[96,1152]{1,0:T(8,128)(2,1)S(1)}, bf16[96,1152]{1,0:T(8,128)(2,1)S(1)}, u32[]{:S(2)}, u32[]{:S(2)}) collective-permute-start(bf16[96,1152]{1,0:T(8,128)(2,1)S(1)} %get-tuple-element.106), channel_id=1, source_target_pairs={{0,2},{2,0},{4,6},{6,4},{8,10},{10,8},{12,14},{14,12},{16,18},{18,... | collective-permute-start | bytes 663560 | tf_op jit(solution)/shard_map/ppermute | solution.py:427
  25.5 13.3 %collective-permute-start.8 = (bf16[96,1152]{1,0:T(8,128)(2,1)S(1)}, bf16[96,1152]{1,0:T(8,128)(2,1)S(1)}, u32[]{:S(2)}, u32[]{:S(2)}) collective-permute-start(bf16[96,1152]{1,0:T(8,128)(2,1)S(1)} %get-tuple-element.106), channel_id=1, source_target_pairs={{0,6},{2,4},{4,2},{6,0},{8,14},{10,12},{12,10},{14,8},{16,22},{18,... | collective-permute-start | bytes 663560 | tf_op jit(solution)/shard_map/ppermute | solution.py:427
  27.0 11.7 %collective-permute-start.7 = (bf16[96,1152]{1,0:T(8,128)(2,1)S(1)}, bf16[96,1152]{1,0:T(8,128)(2,1)S(1)}, u32[]{:S(2)}, u32[]{:S(2)}) collective-permute-start(bf16[96,1152]{1,0:T(8,128)(2,1)S(1)} %get-tuple-element.106), channel_id=1, source_target_pairs={{0,4},{2,6},{4,0},{6,2},{8,12},{10,14},{12,8},{14,10},{16,20},{18,... | collective-permute-start | bytes 663560 | tf_op jit(solution)/shard_map/ppermute | solution.py:427
  98.1 89.4 %collective-permute-start.10 = (bf16[2,256,384]{2,1,0:T(8,128)(2,1)}, bf16[2,256,384]{2,1,0:T(8,128)(2,1)}, u32[]{:S(2)}, u32[]{:S(2)}) collective-permute-start(bf16[2,256,384]{2,1,0:T(8,128)(2,1)} %bitcast.152), channel_id=1, source_target_pairs={{0,1},{1,0},{2,3},{3,2},{4,5},{5,4},{6,7},{7,6},{8,9},{9,8},{10,11... | collective-permute-start | bytes 1179656 | tf_op jit(solution)/shard_map/ppermute | solution.py:424
  123.5 21.5 %collective-permute-start.14 = (f32[16,216]{1,0:T(8,128)S(1)}, f32[16,216]{1,0:T(8,128)S(1)}, u32[]{:S(2)}, u32[]{:S(2)}) collective-permute-start(f32[16,216]{1,0:T(8,128)S(1)} %concatenate.81), channel_id=1, source_target_pairs={{0,1},{1,0},{2,3},{3,2},{4,5},{5,4},{6,7},{7,6},{8,9},{9,8},{10,11... | collective-permute-start | bytes 41480 | tf_op jit(solution)/shard_map/ppermute | solution.py:424
  123.8 21.8 %collective-permute-start.12 = (bf16[16,1152]{1,0:T(8,128)(2,1)S(1)}, bf16[16,1152]{1,0:T(8,128)(2,1)S(1)}, u32[]{:S(2)}, u32[]{:S(2)}) collective-permute-start(bf16[16,1152]{1,0:T(8,128)(2,1)S(1)} %fusion.20), channel_id=1, source_target_pairs={{0,1},{1,0},{2,3},{3,2},{4,5},{5,4},{6,7},{7,6},{8,9},{9,8},{10,11... | collective-permute-start | bytes 110600 | tf_op jit(solution)/shard_map/ppermute | solution.py:424
  131.6 51.4 %collective-permute-start.27 = (bf16[16,48,384]{2,1,0:T(8,128)(2,1)S(1)}, bf16[16,48,384]{2,1,0:T(8,128)(2,1)}, u32[]{:S(2)}, u32[]{:S(2)}) collective-permute-start(bf16[16,48,384]{2,1,0:T(8,128)(2,1)S(1)} %fusion.3), channel_id=1, source_target_pairs={{0,1},{1,0},{2,3},{3,2},{4,5},{5,4},{6,7},{7,6},{8,9},{9,8},{10,11... | collective-permute-start | bytes 1769480 | tf_op jit(solution)/shard_map/ppermute | solution.py:424
  160.6 9.2 %collective-permute-start.23 = (bf16[4,24,1152]{2,1,0:T(8,128)(2,1)}, bf16[4,24,1152]{2,1,0:T(8,128)(2,1)S(1)}, u32[]{:S(2)}, u32[]{:S(2)}) collective-permute-start(bf16[4,24,1152]{2,1,0:T(8,128)(2,1)} %bitcast.33), channel_id=1, source_target_pairs={{0,6},{2,4},{4,2},{6,0},{8,14},{10,12},{12,10},{14,8},{16,22},{18,... | collective-permute-start | bytes 663560 | tf_op jit(solution)/shard_map/ppermute | solution.py:427
  162.8 9.3 %collective-permute-start.21 = (bf16[4,24,1152]{2,1,0:T(8,128)(2,1)}, bf16[4,24,1152]{2,1,0:T(8,128)(2,1)}, u32[]{:S(2)}, u32[]{:S(2)}) collective-permute-start(bf16[4,24,1152]{2,1,0:T(8,128)(2,1)} %bitcast.31), channel_id=1, source_target_pairs={{0,2},{2,0},{4,6},{6,4},{8,10},{10,8},{12,14},{14,12},{16,18},{18,... | collective-permute-start | bytes 663560 | tf_op jit(solution)/shard_map/ppermute | solution.py:427
  164.3 8.0 %collective-permute-start.22 = (bf16[4,24,1152]{2,1,0:T(8,128)(2,1)}, bf16[4,24,1152]{2,1,0:T(8,128)(2,1)}, u32[]{:S(2)}, u32[]{:S(2)}) collective-permute-start(bf16[4,24,1152]{2,1,0:T(8,128)(2,1)} %bitcast.32), channel_id=1, source_target_pairs={{0,4},{2,6},{4,0},{6,2},{8,12},{10,14},{12,8},{14,10},{16,20},{18,... | collective-permute-start | bytes 663560 | tf_op jit(solution)/shard_map/ppermute | solution.py:427
  178.7 9.6 %collective-permute-start.11 = (bf16[2,256,384]{2,1,0:T(8,128)(2,1)S(1)}, bf16[2,256,384]{2,1,0:T(8,128)(2,1)S(1)}, u32[]{:S(2)}, u32[]{:S(2)}) collective-permute-start(bf16[2,256,384]{2,1,0:T(8,128)(2,1)S(1)} %bitcast.153), channel_id=1, source_target_pairs={{0,1},{1,0},{2,3},{3,2},{4,5},{5,4},{6,7},{7,6},{8,9},{9,8},{10,11... | collective-permute-start | bytes 1179656 | tf_op jit(solution)/shard_map/ppermute | solution.py:424
  181.1 17.8 %collective-permute-start.35 = (bf16[16,96,384]{2,1,0:T(8,128)(2,1)S(1)}, bf16[16,96,384]{2,1,0:T(8,128)(2,1)S(1)}, u32[]{:S(2)}, u32[]{:S(2)}) collective-permute-start(bf16[16,96,384]{2,1,0:T(8,128)(2,1)S(1)} %fusion.1), channel_id=1, source_target_pairs={{0,1},{1,0},{2,3},{3,2},{4,5},{5,4},{6,7},{7,6},{8,9},{9,8},{10,11... | collective-permute-start | bytes 3538952 | tf_op jit(solution)/shard_map/ppermute | solution.py:424
  187.6 7.6 %collective-permute-start.29 = (bf16[4,48,384]{2,1,0:T(8,128)(2,1)S(1)}, bf16[4,48,384]{2,1,0:T(8,128)(2,1)S(1)}, u32[]{:S(2)}, u32[]{:S(2)}) collective-permute-start(bf16[4,48,384]{2,1,0:T(8,128)(2,1)S(1)} %get-tuple-element.80), channel_id=1, source_target_pairs={{0,4},{2,6},{4,0},{6,2},{8,12},{10,14},{12,8},{14,10},{16,20},{18,... | collective-permute-start | bytes 442376 | tf_op jit(solution)/shard_map/ppermute | solution.py:427
  195.5 8.4 %collective-permute-start.33 = (bf16[48,384]{1,0:T(8,128)(2,1)S(1)}, bf16[48,384]{1,0:T(8,128)(2,1)S(1)}, u32[]{:S(2)}, u32[]{:S(2)}) collective-permute-start(bf16[48,384]{1,0:T(8,128)(2,1)S(1)} %get-tuple-element.94), channel_id=1, source_target_pairs={{0,24},{2,26},{4,28},{6,30},{8,16},{10,18},{12,20},{14,22},{16,8},... | collective-permute-start | bytes 110600 | tf_op jit(solution)/shard_map/ppermute | solution.py:430
  199.4 10.0 %collective-permute-start.36 = (bf16[4,96,384]{2,1,0:T(8,128)(2,1)S(1)}, bf16[4,96,384]{2,1,0:T(8,128)(2,1)S(1)}, u32[]{:S(2)}, u32[]{:S(2)}) collective-permute-start(bf16[4,96,384]{2,1,0:T(8,128)(2,1)S(1)} %get-tuple-element.68), channel_id=1, source_target_pairs={{0,2},{2,0},{4,6},{6,4},{8,10},{10,8},{12,14},{14,12},{16,18},{18,... | collective-permute-start | bytes 884744 | tf_op jit(solution)/shard_map/ppermute | solution.py:427
  200.4 12.7 %collective-permute-start.38 = (bf16[4,96,384]{2,1,0:T(8,128)(2,1)S(1)}, bf16[4,96,384]{2,1,0:T(8,128)(2,1)S(1)}, u32[]{:S(2)}, u32[]{:S(2)}) collective-permute-start(bf16[4,96,384]{2,1,0:T(8,128)(2,1)S(1)} %get-tuple-element.69), channel_id=1, source_target_pairs={{0,6},{2,4},{4,2},{6,0},{8,14},{10,12},{12,10},{14,8},{16,22},{18,... | collective-permute-start | bytes 884744 | tf_op jit(solution)/shard_map/ppermute | solution.py:427
  201.7 12.8 %collective-permute-start.37 = (bf16[4,96,384]{2,1,0:T(8,128)(2,1)S(1)}, bf16[4,96,384]{2,1,0:T(8,128)(2,1)S(1)}, u32[]{:S(2)}, u32[]{:S(2)}) collective-permute-start(bf16[4,96,384]{2,1,0:T(8,128)(2,1)S(1)} %get-tuple-element.70), channel_id=1, source_target_pairs={{0,4},{2,6},{4,0},{6,2},{8,12},{10,14},{12,8},{14,10},{16,20},{18,... | collective-permute-start | bytes 884744 | tf_op jit(solution)/shard_map/ppermute | solution.py:427
  204.0 14.3 %collective-permute-start.34 = (f32[48,384]{1,0:T(8,128)S(1)}, f32[48,384]{1,0:T(8,128)S(1)}, u32[]{:S(2)}, u32[]{:S(2)}) collective-permute-start(f32[48,384]{1,0:T(8,128)S(1)} %fusion.17), channel_id=1, source_target_pairs={{0,1},{1,0},{2,3},{3,2},{4,5},{5,4},{6,7},{7,6},{8,9},{9,8},{10,11... | collective-permute-start | bytes 221192 | tf_op jit(solution)/shard_map/ppermute | solution.py:424
  (43 other events, 456.7 us)

commit v2 on v1

--- a/solution.py
+++ b/solution.py
@@ -20,6 +20,8 @@
 PAIR = 2 * HEAD_DIM
 TOK = 256
 FCH = 256
+LANES = 128
+INNER = 4
 GELU_A = math.sqrt(2.0 / math.pi)
 GELU_B = 0.044715
 F32 = jnp.float32
@@ -75,13 +77,86 @@
     return jnp.where((lane // HEAD_DIM) == half, values, jnp.zeros_like(values))
 
 
-def forward_kernel(
+FWD_IN = (
+    "place",
+    "tok_own",
+    "tok_in",
+    "cot_own",
+    "cot_in",
+    "row",
+    "mod",
+    "head_tab",
+    "chan_tab",
+    "w_qkv",
+    "b_qv",
+    "w_proj",
+    "b_proj",
+    "w_fc1",
+    "b_fc1",
+    "w_fc2",
+    "b_fc2",
+    "w_router",
+)
+FWD_OUT = (
+    "out_own",
+    "out_far",
+    "hid_out",
+    "q_out",
+    "k_out",
+    "v_out",
+    "prob_out",
+    "gheads_out",
+    "gres_out",
+    "dwp",
+    "gmod",
+)
+FWD_FAST = ("e_own", "e_send", "parcel", "gme_own", "gme_send")
+FWD_SUMS = ("dw1", "dw2", "db2", "dwr")
+FWD_TEMP = (
+    "x_s",
+    "cot_s",
+    "bias_s",
+    "hot_s",
+    "tab_s",
+    "mix_s",
+    "att_s",
+    "branch_s",
+    "res_s",
+    "h2_s",
+    "coef_s",
+    "gml_s",
+    "mlp_s",
+    "gh2_s",
+    "gm_s",
+    "col_s",
+)
+
+
+def named_call(kernel, refs):
+    wanted = kernel.__code__.co_varnames[: kernel.__code__.co_argcount]
+    kernel(*[refs[name] for name in wanted])
+
+
+def forward_kernel(fast, *refs):
+    names = FWD_IN + FWD_OUT
+    names += FWD_FAST + FWD_TEMP + FWD_SUMS if fast else FWD_SUMS + FWD_TEMP
+    refs = dict(zip(names, refs, strict=True))
+    named_call(forward_row, refs)
+    if fast:
+
+        @pl.when(pl.program_id(0) == pl.num_programs(0) - 1)
+        def _():
+            named_call(forward_flush, refs)
+
+        named_call(forward_mod, refs)
+
+
+def forward_row(
     place,
     tok_own,
     tok_in,
     cot_own,
     cot_in,
-    col,
     row,
     mod,
     head_tab,
@@ -104,14 +179,12 @@
     prob_out,
     gheads_out,
     gres_out,
+    dwp,
+    gmod,
     dw1,
     dw2,
-    dwp,
-    db1,
     db2,
-    dbp,
     dwr,
-    gmod,
     x_s,
     cot_s,
     bias_s,
@@ -127,6 +200,7 @@
     mlp_s,
     gh2_s,
     gm_s,
+    col_s,
 ):
     length = x_s.shape[0]
     local = tok_own.shape[1]
@@ -134,8 +208,10 @@
 
     @pl.when(pl.program_id(0) == 0)
     def _():
-        for ref in (dw1, dw2, dwp, db1, db2, dbp, dwr):
+        for ref in (dw1, dw2, dwp, db2, dwr):
             ref[...] = jnp.zeros_like(ref)
+        for ref in (att_s, h2_s):
+            ref[:, D:] = jnp.ones((length, LANES), BF16)
 
     x_s[0:local] = tok_own[0].astype(F32)
     cot_s[0:local] = cot_own[0].astype(F32)
@@ -147,12 +223,13 @@
     gh2_s[...] = jnp.zeros_like(gh2_s)
     gm_s[...] = jnp.zeros_like(gm_s)
     id_row = row[0, 0:1, :]
+    col_s[...] = row[0].T
 
     def first(i, _):
         part = pl.ds(i * TOK, TOK)
-        hot = crop_rows(col[0, part, 0:1], TOK)
+        hot = crop_rows(col_s[part, 1:2], TOK)
         hot_s[part] = hot
-        bias_s[part] = jnp.where(col[0, part, 1:2] == id_row, 0.0, NEGATIVE)
+        bias_s[part] = jnp.where(col_s[part, 0:1] == id_row, 0.0, NEGATIVE)
         normal, _ = normalise(x_s[part])
         hidden = (normal * (1.0 + dot(hot, tab_s[:, D : 2 * D])) + dot(hot, tab_s[:, 0:D])).astype(
             BF16
@@ -193,8 +270,8 @@
     def middle(i, _):
         part = pl.ds(i * TOK, TOK)
         hot = hot_s[part]
-        live = jnp.where(col[0, part, 1:2] >= 0.0, 1.0, 0.0)
-        branch = dot(att_s[part], w_proj[...]) + b_proj[...]
+        live = jnp.where(col_s[part, 0:1] >= 0.0, 1.0, 0.0)
+        branch = dot(att_s[part, 0:D], w_proj[...]) + b_proj[...]
         branch_s[part] = branch
         residual = x_s[part] + live * dot(hot, tab_s[:, 2 * D : 3 * D]) * branch
         res_s[part] = residual
@@ -202,16 +279,16 @@
         hidden = (
             normal * (1.0 + dot(hot, tab_s[:, 4 * D : 5 * D])) + dot(hot, tab_s[:, 3 * D : 4 * D])
         ).astype(BF16)
-        h2_s[part] = hidden
+        h2_s[part, 0:D] = hidden
         logit = jnp.sum(hidden.astype(F32) * w_router[...], -1, keepdims=True)
         rate = 1.0 / (1.0 + jnp.exp(-logit))
-        keep = live * col[0, part, 2:3]
+        keep = live * col_s[part, 2:3]
         coef = keep * rate
         coef_s[part, 0:1] = coef
         coef_s[part, 1:2] = coef * (1.0 - rate)
         gml = (cot_s[part] * coef * dot(hot, tab_s[:, 5 * D : 6 * D])).astype(BF16)
         gml_s[part] = gml
-        db2[...] += jnp.sum(gml.astype(F32), 0, keepdims=True)
+        db2[...] += dot_tn(gml, jnp.ones((TOK, LANES), BF16))
         return 0
 
     lax.fori_loop(0, length // TOK, middle, 0)
@@ -219,7 +296,7 @@
     def feed(c, _):
         units = pl.ds(pl.multiple_of(c * FCH, FCH), FCH)
         hidden, gml = h2_s[...], gml_s[...]
-        pre = dot(hidden, w_fc1[:, units]) + b_fc1[:, units]
+        pre = dot(hidden[:, 0:D], w_fc1[:, units]) + b_fc1[:, units]
         mask = dot(hot_s[...], chan_tab[0, :, units])
         square = pre * pre
         tanh = jnp.tanh(pre * (GELU_A + (GELU_A * GELU_B) * square))
@@ -231,7 +308,6 @@
         dw2[units, :] += dot_tn(act, gml)
         gpre = (slope * mask * dot_nt(gml, w_fc2[units, :])).astype(BF16)
         dw1[units, :] += dot_tn(gpre, hidden)
-        db1[:, units] += jnp.sum(gpre.astype(F32), 0, keepdims=True)
         gh2_s[...] += dot_nt(gpre, w_fc1[:, units])
         return 0
 
@@ -240,7 +316,7 @@
     def last(i, _):
         part = pl.ds(i * TOK, TOK)
         hot = hot_s[part]
-        live = jnp.where(col[0, part, 1:2] >= 0.0, 1.0, 0.0)
+        live = jnp.where(col_s[part, 0:1] >= 0.0, 1.0, 0.0)
         coef = coef_s[part, 0:1]
         cot = cot_s[part]
         mlp = mlp_s[part] + b_fc2[...]
@@ -250,8 +326,10 @@
         mlp_s[part] = outcome.astype(F32)
         cot_mlp = cot * mlp
         grad_logit = jnp.sum(cot_mlp * gate2, -1, keepdims=True) * coef_s[part, 1:2]
-        hidden = h2_s[part].astype(F32)
-        dwr[...] += jnp.sum(hidden * grad_logit, 0, keepdims=True)
+        logit_high = grad_logit.astype(BF16).astype(F32)
+        lane = lax.broadcasted_iota(jnp.int32, (TOK, LANES), 1)
+        logit_terms = jnp.where(lane < LANES // 2, logit_high, grad_logit - logit_high)
+        dwr[...] += dot_tn(h2_s[part, 0:D], logit_terms.astype(BF16))
         grad_hidden = gh2_s[part] + grad_logit * w_router[...]
         normal, inverse = normalise(residual)
         grad_res = cot + normalise_back(
@@ -265,7 +343,6 @@
         gm_s[:, D : 2 * D] += dot(hot_t, grad_hidden.astype(BF16))
         gm_s[:, 2 * D : 3 * D] += dot(hot_t, (grad_hidden * normal).astype(BF16))
         gm_s[:, 3 * D : 4 * D] += dot(hot_t, (cot_mlp * coef).astype(BF16))
-        dbp[...] += jnp.sum(grad_branch.astype(F32), 0, keepdims=True)
         dwp[...] += dot_tn(grad_branch, att_s[part])
         gheads_out[0, part] = (
             dot_nt(grad_branch, w_proj[...]).astype(BF16).astype(F32) * dot(hot, head_tab[0])
@@ -279,11 +356,131 @@
     gmod[0] = gm_s[0:CROPS]
 
 
-def backward_kernel(
+def lane_put(lane, column):
+    position = lax.broadcasted_iota(jnp.int32, (column.shape[0], LANES), 1)
+    return jnp.where(position == lane, column, 0.0)
+
+
+def slot_of(near, inner, outer):
+    return (near & (inner - 1)) * outer + near // inner
+
+
+def forward_flush(place, dw1, dw2, dwp, db2, dwr, e_own, e_send, parcel):
+    buckets, units, _ = e_own.shape
+    depth = parcel.shape[1]
+
+    def one(b, _):
+        slot = slot_of(b ^ place[1], INNER, buckets // INNER)
+        rows = pl.ds(pl.multiple_of(b * units, 8), units)
+        first, second = dw1[rows, 0:D], dw2[rows, :]
+        swap = place[0] == 0
+        e_own[slot] = jnp.where(swap, first, second)
+        e_send[slot] = jnp.where(swap, second, first).astype(BF16)
+        held = jnp.zeros((depth, LANES), F32)
+        for i in range(units // depth):
+            held += lane_put(
+                i, dw1[pl.ds(pl.multiple_of(b * units + i * depth, 8), depth), D : D + 1]
+            )
+        part = pl.ds(pl.multiple_of(b * depth, 8), depth)
+        count = units // depth
+        held += lane_put(count, db2[part, 0:1])
+        held += lane_put(count + 1, dwp[part, D : D + 1])
+        held += lane_put(count + 2, dwr[part, 0:1] + dwr[part, LANES // 2 : LANES // 2 + 1])
+        parcel[slot] = held
+        return 0
+
+    lax.fori_loop(0, buckets, one, 0)
+
+
+def forward_mod(place, gm_s, gme_own, gme_send):
+    first, second = gm_s[0:CROPS, 0:D], gm_s[0:CROPS, D : 2 * D]
+    swap = place[0] == 0
+    gme_own[0] = jnp.where(swap, first, second)
+    gme_send[0] = jnp.where(swap, second, first)
+
+
+BWD_IN = (
+    "place",
+    "tok_own",
+    "tok_in",
+    "row",
+    "mod",
+    "w_qkv",
+    "hid",
+    "q_in",
+    "k_in",
+    "v_in",
+    "prob_in",
+    "gheads",
+    "gres",
+)
+BWD_FAST_IN = ("dwp", "parcel_in", "gm_in")
+BWD_OUT = ("gt_own", "gt_far")
+BWD_FAST = ("l_own", "l_send", "parcel", "gml_own", "gml_send")
+BWD_TEMP = ("gp_s", "dk_s", "dv_s", "dq_s", "x_s", "tab_s", "hid_s", "gm_s", "col_s")
+
+
+def backward_kernel(fast, *refs):
+    names = BWD_IN
+    if fast:
+        names += BWD_FAST_IN + BWD_OUT + BWD_FAST + BWD_TEMP + ("dwq",)
+    else:
+        names += BWD_OUT + ("dwq", "gmod") + BWD_TEMP
+    refs = dict(zip(names, refs, strict=True))
+    named_call(backward_row, refs)
+    if not fast:
+        refs["gmod"][0] = refs["gm_s"][0:CROPS]
+        return
+
+    @pl.when(pl.program_id(0) == pl.num_programs(0) - 1)
+    def _():
+        named_call(backward_flush, refs)
+
+    named_call(backward_mod, refs)
+
+
+def backward_mod(place, gm_s, gm_in, gml_own, gml_send):
+    first, second = gm_s[0:CROPS], gm_in[0, :, 2 * D :]
+    swap = place[0] == 0
+    gml_own[0] = jnp.where(swap, first, second)
+    gml_send[0] = jnp.where(swap, second, first)
+
+
+def backward_flush(place, dwq, dwp, parcel_in, l_own, l_send, parcel):
+    buckets, lines, _ = l_own.shape
+    depth = parcel.shape[1]
+
+    def one(b, _):
+        slot = slot_of(b ^ place[1], INNER, buckets // INNER)
+        start = b * 3 * depth
+        first = dwq[pl.ds(pl.multiple_of(start, 8), lines), 0:D]
+        second = jnp.concatenate(
+            [
+                dwq[pl.ds(pl.multiple_of(start + lines, 8), 3 * depth - lines), 0:D],
+                dwp[pl.ds(pl.multiple_of(b * depth, 8), depth), 0:D],
+            ],
+            0,
+        )
+        swap = place[0] == 0
+        l_own[slot] = jnp.where(swap, first, second)
+        l_send[slot] = jnp.where(swap, second, first).astype(BF16)
+        held = parcel_in[slot]
+        start = b * 2 * depth
+        start = jnp.where(start < D, start, start + D)
+        for i in range(2):
+            held += lane_put(
+                7 + i, dwq[pl.ds(pl.multiple_of(start + i * depth, 8), depth), D : D + 1]
+            )
+        parcel[slot] = held
+        return 0
+
+    lax.fori_loop(0, buckets, one, 0)
+
+
+def backward_row(
     place,
     tok_own,
     tok_in,
-    col,
     row,
     mod,
     w_qkv,
@@ -297,15 +494,15 @@
     gt_own,
     gt_far,
     dwq,
-    dbq,
-    gmod,
     gp_s,
     dk_s,
     dv_s,
     dq_s,
     x_s,
     tab_s,
+    hid_s,
     gm_s,
+    col_s,
 ):
     length = x_s.shape[0]
     local = tok_own.shape[1]
@@ -313,13 +510,14 @@
 
     @pl.when(pl.program_id(0) == 0)
     def _():
-        for ref in (dwq, dbq):
-            ref[...] = jnp.zeros_like(ref)
+        dwq[...] = jnp.zeros_like(dwq)
+        hid_s[:, D:] = jnp.ones((length, LANES), BF16)
 
     x_s[0:local] = tok_own[0].astype(F32)
     for j in range(far):
         x_s[(j + 1) * local : (j + 2) * local] = tok_in[j, 0].astype(F32)
     tab_s[...] = three_terms(mod[0, :, D : 2 * D])
+    col_s[...] = row[0].T
     gm_s[...] = jnp.zeros_like(gm_s)
 
     def attend(hp, _):
@@ -353,9 +551,8 @@
 
     def last(i, _):
         part = pl.ds(i * TOK, TOK)
-        hot = crop_rows(col[0, part, 0:1], TOK)
+        hot = crop_rows(col_s[part, 1:2], TOK)
         grad = gp_s[part]
-        dbq[...] += jnp.sum(grad.astype(F32), 0, keepdims=True)
         grad_hidden = dot_nt(grad, w_qkv[...])
         normal, inverse = normalise(x_s[part])
         hot_t = crop_columns(row[0, 1:2, part], TOK)
@@ -367,13 +564,200 @@
         return 0
 
     lax.fori_loop(0, length // TOK, last, 0)
+    hid_s[:, 0:D] = hid[0]
     for c in range(3):
         rows = slice(c * D, (c + 1) * D)
-        dwq[rows, :] += dot_tn(gp_s[:, rows], hid[0])
+        dwq[rows, :] += dot_tn(gp_s[:, rows], hid_s[...])
     gt_own[0] = x_s[0:local].astype(BF16)
     for j in range(far):
         gt_far[j, 0] = x_s[(j + 1) * local : (j + 2) * local].astype(BF16)
-    gmod[0] = gm_s[0:CROPS]
+
+
+def seq_order(place, own, far):
+    own, far = own.reshape(-1, own.shape[-1]), far.reshape(-1, far.shape[-1])
+    return jnp.where(
+        place[0] == 0, jnp.concatenate([own, far], 0), jnp.concatenate([far, own], 0)
+    ).astype(BF16)
+
+
+def early_pack(place, e_own, e_in, gm_own, gm_in, silu, keep, *sends):
+    outer = keep.shape[0]
+    depth = D // e_own.shape[0]
+    ada = dot_tn(silu[...], seq_order(place, gm_own[...], gm_in[...]))
+    for slot in range(e_own.shape[0]):
+        total = jnp.concatenate(
+            [e_own[slot] + e_in[slot].astype(F32), ada[slot * depth : (slot + 1) * depth]], 0
+        )
+        if slot < outer:
+            keep[slot] = total
+        else:
+            sends[slot // outer - 1][slot % outer] = total.astype(BF16)
+
+
+def early_line(own, in1, in2, in3, keep, *sends):
+    for k in range(own.shape[0]):
+        total = own[k] + in1[k].astype(F32) + in2[k].astype(F32) + in3[k].astype(F32)
+        if k == 0:
+            keep[...] = total
+        else:
+            sends[k - 1][...] = total.astype(BF16)
+
+
+def late_pack(
+    place,
+    l_own,
+    l_in,
+    gml_own,
+    gml_in,
+    gme_own,
+    gme_in,
+    silu,
+    ada,
+    slope,
+    ids,
+    parcel,
+    keep,
+    s1,
+    s2,
+    s3,
+    gm_s,
+    ada_s,
+):
+    sends = (s1, s2, s3)
+    outer = keep.shape[0]
+    buckets, lines, _ = l_own.shape
+    depth = D // buckets
+    crops = silu.shape[0]
+    late = seq_order(place, gml_own[...], gml_in[...])
+    early = seq_order(place, gme_own[...], gme_in[...])
+    gm_s[...] = jnp.zeros_like(gm_s)
+
+    @pl.when(place[0] == 0)
+    def _():
+        gm_s[crops : 2 * crops, 0 : 2 * D] = late
+        gm_s[crops : 2 * crops, 2 * D :] = early
+
+    @pl.when(place[0] != 0)
+    def _():
+        gm_s[crops : 2 * crops, 0:D] = early
+        gm_s[crops : 2 * crops, D:] = late
+
+    grads = dot_tn(silu[...], late)
+    crop_t = dot_nt(ada[...], gm_s[...]) * slope[...]
+    ada_s[...] = dot_tn(gm_s[...], jnp.ones((LANES, LANES), BF16))
+    for slot in range(buckets):
+        bucket = place[1] ^ ((slot // outer) + INNER * (slot % outer))
+        held = parcel[slot] + crop_t[slot * depth : (slot + 1) * depth] + ids[...]
+        for i in range(3):
+            start = pl.multiple_of(bucket * 3 * depth + i * depth, 8)
+            held += lane_put(9 + i, ada_s[pl.ds(start, depth), 0:1])
+        part = slice(slot * depth, (slot + 1) * depth)
+        total = jnp.concatenate(
+            [
+                l_own[slot] + l_in[slot].astype(F32),
+                grads[part, 0:D],
+                grads[part, D:],
+                jnp.concatenate([held[8 * i : 8 * (i + 1)] for i in range(3)], 1),
+            ],
+            0,
+        )
+        if slot < outer:
+            keep[slot] = total
+        else:
+            sends[slot // outer - 1][slot % outer] = total.astype(BF16)
+
+
+def late_line(own, in1, in2, in3, keep, *sends):
+    sums = own.shape[1] - 8
+    for k in range(own.shape[0]):
+        pieces = [own[k]] + [piece[k].astype(F32) for piece in (in1, in2, in3)]
+        total = pieces[0][0:sums]
+        for piece in pieces[1:]:
+            total = total + piece[0:sums]
+        total = jnp.concatenate([total] + [piece[sums:] for piece in pieces], 0)
+        if k == 0:
+            keep[...] = total
+        else:
+            sends[k - 1][...] = total.astype(BF16)
+
+
+def last_pack(place, early, e1, e2, e3, late, l1, l2, l3, parts, ada):
+    depth = ada.shape[0]
+    units = early.shape[0] - depth
+    e_sum = early[...] + e1[...].astype(F32) + e2[...].astype(F32) + e3[...].astype(F32)
+    pieces = [late[...]] + [piece[...].astype(F32) for piece in (l1, l2, l3)]
+    sums = late.shape[0] - 8 * INNER
+    lines = sums - 2 * depth
+    l_sum = pieces[0][0:sums]
+    for piece in pieces[1:]:
+        l_sum = l_sum + piece[0:sums]
+    parts[0:units] = e_sum[0:units]
+    parts[units : units + lines] = l_sum[0:lines]
+    for i, piece in enumerate(pieces):
+        start = units + lines + 8 * INNER * i
+        parts[start : start + 8 * INNER] = piece[sums:]
+    tail, first, second = e_sum[units:], l_sum[lines : lines + depth], l_sum[lines + depth :]
+    swap = place[0] == 0
+    ada[:, 0:D] = jnp.where(swap, first, tail)
+    ada[:, D : 2 * D] = jnp.where(swap, second, first)
+    ada[:, 2 * D :] = jnp.where(swap, tail, second)
+
+
+def spread(columns, depth):
+    line = lax.broadcasted_iota(jnp.int32, (depth, LANES), 0)
+    lane = lax.broadcasted_iota(jnp.int32, (depth, LANES), 1)
+    total = jnp.zeros((depth, LANES), F32)
+    for i, column in enumerate(columns):
+        total += jnp.where(lane - depth * i == line, column, 0.0)
+    return jnp.sum(total, 0, keepdims=True)
+
+
+def finish(
+    place, own, far, table, qkv, qv, proj, bp, fc1, b1, fc2, b2, router, b_ada, crop_s, hot_s
+):
+    units, depth = fc2.shape[0], router.shape[1]
+    lines = 4 * depth // 2
+    swap = place[0] == 0
+    own_e, far_e = own[0:units], far[0:units]
+    fc1[...] = jnp.where(swap, own_e, far_e)
+    fc2[...] = jnp.where(swap, far_e, own_e)
+    own_l, far_l = own[units : units + lines], far[units : units + lines]
+    first, second = jnp.where(swap, own_l, far_l), jnp.where(swap, far_l, own_l)
+    cut = 3 * depth - lines
+    qkv[...] = jnp.concatenate([first, second[0:cut]], 0)
+    proj[...] = second[cut:]
+    own_sum = jnp.zeros((depth, LANES), F32)
+    far_sum = jnp.zeros((depth, LANES), F32)
+    sources = (own.shape[0] - units - lines) // 8
+    wide = lax.broadcasted_iota(jnp.int32, (32, hot_s.shape[1]), 1).astype(F32)
+    for source in range(sources):
+        rows = slice(units + lines + 8 * source, units + lines + 8 * (source + 1))
+        own_p = jnp.concatenate([own[rows, i * LANES : (i + 1) * LANES] for i in range(3)], 0)
+        far_p = jnp.concatenate([far[rows, i * LANES : (i + 1) * LANES] for i in range(3)], 0)
+        own_sum += own_p
+        far_sum += far_p
+        both = (own_p + far_p).T
+        grads = both[32:64]
+        high = grads.astype(BF16).astype(F32)
+        crops = slice(32 * source, 32 * (source + 1))
+        crop_s[crops, 0:depth] = high
+        crop_s[crops, 32 : 32 + depth] = grads - high
+        ids = own_p.T
+        crop_id = ids[64:96, 0:1] * 8.0 + ids[96:128, 0:1]
+        hot_s[crops] = jnp.where(crop_id == wide, 1.0, 0.0).astype(BF16)
+    terms = dot_tn(crop_s[:, 0:64].astype(BF16), hot_s[...])
+    table[...] = (terms[0:depth] + terms[32 : 32 + depth])[:, 0 : table.shape[1]]
+    total = own_sum + far_sum
+
+    def lane(values, i):
+        return values[:, i : i + 1]
+
+    b1[...] = spread([lane(total, i) for i in range(4)], depth)[:, 0:units]
+    b2[...] = spread([lane(total, 4)], depth)[:, 0:depth]
+    bp[...] = spread([lane(total, 5)], depth)[:, 0:depth]
+    router[...] = spread([lane(total, 6)], depth)[:, 0:depth]
+    qv[...] = spread([lane(total, 7), lane(total, 8)], depth)[:, 0 : 2 * depth]
+    b_ada[...] = spread([lane(own_sum, 9 + i) for i in range(3)], depth)[:, 0 : 3 * depth]
 
 
 def whole(shape):
@@ -458,8 +842,7 @@
         [lax.dynamic_slice_in_dim(both, (me_s ^ j) * local, local, 2) for j in range(seqs)], 2
     )
     keep_all = jnp.concatenate([slab(keep_mask, me_s, mine)] + keep_in, 1).astype(F32)
-    col = jnp.stack([both[0], both[1], keep_all, keep_all], -1)
-    row = jnp.stack([both[1], both[0]], 1)
+    row = jnp.stack([both[1], both[0], keep_all, keep_all], 1)
 
     half_width = D // 2
     frequency = jnp.exp(-math.log(10000.0) * jnp.arange(half_width, dtype=F32) / half_width)
@@ -493,7 +876,7 @@
 
     head_tab = table_of(slab(head_mask, me_s, mine), HEAD_DIM)
     chan_tab = table_of(slab(channel_mask, me_s, mine), FF // CGROUPS)
-    place = me_s.reshape(1).astype(jnp.int32)
+    place = jnp.stack([me_s, me_b]).astype(jnp.int32)
     own = pl.BlockSpec((1, local, D), lambda r, place: (place[0] * mine + r, 0, 0))
     far = seqs - 1
     bias_row = bias_qv.astype(F32).reshape(1, 2 * D)
@@ -501,44 +884,60 @@
     def struct(shape, kind=F32):
         return jax.ShapeDtypeStruct(shape, kind)
 
-    fwd_shapes = [
-        struct((mine, local, D), BF16),
-        struct((far, mine, local, D), BF16),
-        struct((mine, length, D), BF16),
-        struct((mine, length, D), BF16),
-        struct((mine, length, D), BF16),
-        struct((mine, length, D), BF16),
-        struct((mine, HEADS, length, length), BF16),
-        struct((mine, length, D), BF16),
-        struct((mine, length, D)),
-        struct((FF, D)),
-        struct((FF, D)),
-        struct((D, D)),
-        struct((1, FF)),
-        struct((1, D)),
-        struct((1, D)),
-        struct((1, D)),
-        struct((mine, CROPS, 4 * D)),
+    lanes = LANES
+    fast = (
+        seqs == 2 and buckets == 16 and crops_here == 4 * CROPS and (FF // buckets) % (4 * depth) == 0
+    )
+    if fast:
+        slope_t = jnp.pad(slope_near.T, ((0, 0), (crops_here, lanes - 2 * crops_here)))
+        id_lanes = jnp.pad(
+            jnp.concatenate([class_ids // 8, class_ids % 8]).astype(F32)[None],
+            ((0, depth - 1), (lanes - 2 * crops_here, 0)),
+        )
+    sum_shapes = [(FF, D + lanes), (FF, D), (D, lanes), (D, lanes)]
+    out_names = [
+        (struct((mine, local, D), BF16), per_row((local, D))),
+        (struct((far, mine, local, D), BF16), per_far(far, (local, D))),
     ]
-    fwd_out_specs = [
-        per_row((local, D)),
-        per_far(far, (local, D)),
-        per_row((length, D)),
-        per_row((length, D)),
-        per_row((length, D)),
-        per_row((length, D)),
-        per_row((HEADS, length, length)),
-        per_row((length, D)),
-        per_row((length, D)),
-        whole((FF, D)),
-        whole((FF, D)),
-        whole((D, D)),
-        whole((1, FF)),
-        whole((1, D)),
-        whole((1, D)),
-        whole((1, D)),
-        per_row((CROPS, 4 * D)),
+    out_names += [(struct((mine, length, D), BF16), per_row((length, D)))] * 4
+    out_names += [
+        (struct((mine, HEADS, length, length), BF16), per_row((HEADS, length, length))),
+        (struct((mine, length, D), BF16), per_row((length, D))),
+        (struct((mine, length, D)), per_row((length, D))),
+        (struct((D, D + lanes)), whole((D, D + lanes))),
+        (struct((mine, CROPS, 4 * D)), per_row((CROPS, 4 * D))),
     ]
+    if fast:
+        units = FF // buckets
+        out_names += [
+            (struct((buckets, units, D)), whole((buckets, units, D))),
+            (struct((buckets, units, D), BF16), whole((buckets, units, D))),
+            (struct((buckets, depth, lanes)), whole((buckets, depth, lanes))),
+            (struct((mine, CROPS, D)), per_row((CROPS, D))),
+            (struct((mine, CROPS, D)), per_row((CROPS, D))),
+        ]
+    else:
+        out_names += [(struct(shape), whole(shape)) for shape in sum_shapes]
+    scratch = [
+        pltpu.VMEM((length, D), F32),
+        pltpu.VMEM((length, D), F32),
+        pltpu.VMEM((length, length), F32),
+        pltpu.VMEM((length, 4 * CROPS), BF16),
+        pltpu.VMEM((4 * CROPS, 6 * D), BF16),
+        pltpu.VMEM((PAIR, length), F32),
+        pltpu.VMEM((length, D + lanes), BF16),
+        pltpu.VMEM((length, D), F32),
+        pltpu.VMEM((length, D), F32),
+        pltpu.VMEM((length, D + lanes), BF16),
+        pltpu.VMEM((length, 2), F32),
+        pltpu.VMEM((length, D), BF16),
+        pltpu.VMEM((length, D), F32),
+        pltpu.VMEM((length, D), F32),
+        pltpu.VMEM((2 * CROPS, 4 * D), F32),
+        pltpu.VMEM((length, 4), F32),
+    ]
+    if fast:
+        scratch += [pltpu.VMEM(shape, F32) for shape in sum_shapes]
     tokens_here = mine * length
     (
         out_own,
@@ -550,16 +949,12 @@
         prob,
         grad_heads,
         grad_res,
-        dw1,
-        dw2,
         dwp,
-        db1,
-        db2,
-        dbp,
-        dwr,
         gmod_late,
+        *sums,
     ) = pl.pallas_call(
-        forward_kernel,
+        partial(forward_kernel, fast),
+        name="layer_forward",
         grid_spec=pltpu.PrefetchScalarGridSpec(
             num_scalar_prefetch=1,
             grid=(mine,),
@@ -568,8 +963,7 @@
                 per_far(far, (local, D)),
                 own,
                 per_far(far, (local, D)),
-                per_row((length, 4)),
-                per_row((2, length)),
+                per_row((4, length)),
                 per_row((CROPS, 6 * D)),
                 per_row((4 * CROPS, D)),
                 per_row((4 * CROPS, FF)),
@@ -583,26 +977,10 @@
                 whole((1, D)),
                 whole((1, D)),
             ],
-            out_specs=fwd_out_specs,
-            scratch_shapes=[
-                pltpu.VMEM((length, D), F32),
-                pltpu.VMEM((length, D), F32),
-                pltpu.VMEM((length, length), F32),
-                pltpu.VMEM((length, 4 * CROPS), BF16),
-                pltpu.VMEM((4 * CROPS, 6 * D), BF16),
-                pltpu.VMEM((PAIR, length), F32),
-                pltpu.VMEM((length, D), BF16),
-                pltpu.VMEM((length, D), F32),
-                pltpu.VMEM((length, D), F32),
-                pltpu.VMEM((length, D), BF16),
-                pltpu.VMEM((length, 2), F32),
-                pltpu.VMEM((length, D), BF16),
-                pltpu.VMEM((length, D), F32),
-                pltpu.VMEM((length, D), F32),
-                pltpu.VMEM((2 * CROPS, 4 * D), F32),
-            ],
+            out_specs=[spec for _, spec in out_names],
+            scratch_shapes=scratch,
         ),
-        out_shape=fwd_shapes,
+        out_shape=[shape for shape, _ in out_names],
         cost_estimate=pl.CostEstimate(
             flops=2 * tokens_here * (4 * D * D + 6 * D * FF + 2 * D * length),
             transcendentals=tokens_here * (FF + HEADS * length),
@@ -614,7 +992,6 @@
         tok_in,
         cotangent,
         cot_in,
-        col,
         row,
         modulation,
         head_tab,
@@ -660,75 +1037,197 @@
         return line
 
     output = return_rows(out_own, out_far)
-    early = sum_over_all([dw1, dw2])
-
-    gt_own, gt_far, dwq, dbq, gmod_first = pl.pallas_call(
-        backward_kernel,
+
+    def glue(kernel, shapes, *operands, temps=()):
+        return pl.pallas_call(
+            kernel,
+            name=kernel.__name__,
+            in_specs=[pl.BlockSpec(memory_space=pltpu.SMEM)] * (operands[0] is place)
+            + [pl.BlockSpec(memory_space=pltpu.VMEM)] * (len(operands) - (operands[0] is place)),
+            out_specs=[pl.BlockSpec(memory_space=pltpu.VMEM)] * len(shapes),
+            out_shape=shapes,
+            scratch_shapes=list(temps),
+            cost_estimate=pl.CostEstimate(flops=0, transcendentals=0, bytes_accessed=6_000_000),
+        )(*operands)
+
+    back_in = [
+        (place, None),
+        (tokens, own),
+        (tok_in, per_far(far, (local, D))),
+        (row, per_row((4, length))),
+        (modulation, per_row((CROPS, 6 * D))),
+        (w_qkv, whole((D, 3 * D))),
+        (hid, per_row((length, D))),
+        (query, per_row((length, D))),
+        (key, per_row((length, D))),
+        (value, per_row((length, D))),
+        (prob, per_row((HEADS, length, length))),
+        (grad_heads, per_row((length, D))),
+        (grad_res, per_row((length, D))),
+    ]
+    back_out = [
+        (struct((mine, local, D), BF16), per_row((local, D))),
+        (struct((far, mine, local, D), BF16), per_far(far, (local, D))),
+    ]
+    back_temp = [
+        pltpu.VMEM((length, 3 * D), BF16),
+        pltpu.VMEM((length, PAIR), F32),
+        pltpu.VMEM((length, PAIR), F32),
+        pltpu.VMEM((PAIR, length), F32),
+        pltpu.VMEM((length, D), F32),
+        pltpu.VMEM((4 * CROPS, D), BF16),
+        pltpu.VMEM((length, D + lanes), BF16),
+        pltpu.VMEM((2 * CROPS, 2 * D), F32),
+        pltpu.VMEM((length, 4), F32),
+    ]
+    if fast:
+        lines = 2 * depth
+        e_own, e_send, parcel, gme_own, gme_send = sums
+        e_in, gme_in = seq_hop(e_send, 1), seq_hop(gme_send, 1)
+        early = units + depth
+        keep, *sends = glue(
+            early_pack,
+            [struct((outer, early, D))] + [struct((outer, early, D), BF16)] * 3,
+            place,
+            e_own,
+            e_in,
+            gme_own,
+            gme_in,
+            silu_near,
+        )
+        early_plane = [plane_hop(sends[k - 1], k) for k in range(1, inner)]
+        prob, keep = lax.optimization_barrier((prob, keep))
+        back_in[10] = (prob, back_in[10][1])
+        back_in += [
+            (dwp, whole((D, D + lanes))),
+            (parcel, whole((buckets, depth, lanes))),
+            (gmod_late, per_row((CROPS, 4 * D))),
+        ]
+        back_out += [
+            (struct((buckets, lines, D)), whole((buckets, lines, D))),
+            (struct((buckets, lines, D), BF16), whole((buckets, lines, D))),
+            (struct((buckets, depth, lanes)), whole((buckets, depth, lanes))),
+            (struct((mine, CROPS, 2 * D)), per_row((CROPS, 2 * D))),
+            (struct((mine, CROPS, 2 * D)), per_row((CROPS, 2 * D))),
+        ]
+        back_temp.append(pltpu.VMEM((3 * D, D + lanes), F32))
+    else:
+        back_out += [
+            (struct((3 * D, D + lanes)), whole((3 * D, D + lanes))),
+            (struct((mine, CROPS, 2 * D)), per_row((CROPS, 2 * D))),
+        ]
+    gt_own, gt_far, *rest = pl.pallas_call(
+        partial(backward_kernel, fast),
+        name="layer_backward",
         grid_spec=pltpu.PrefetchScalarGridSpec(
             num_scalar_prefetch=1,
             grid=(mine,),
-            in_specs=[
-                own,
-                per_far(far, (local, D)),
-                per_row((length, 4)),
-                per_row((2, length)),
-                per_row((CROPS, 6 * D)),
-                whole((D, 3 * D)),
-                per_row((length, D)),
-                per_row((length, D)),
-                per_row((length, D)),
-                per_row((length, D)),
-                per_row((HEADS, length, length)),
-                per_row((length, D)),
-                per_row((length, D)),
-            ],
-            out_specs=[
-                per_row((local, D)),
-                per_far(far, (local, D)),
-                whole((3 * D, D)),
-                whole((1, 3 * D)),
-                per_row((CROPS, 2 * D)),
-            ],
-            scratch_shapes=[
-                pltpu.VMEM((length, 3 * D), BF16),
-                pltpu.VMEM((length, PAIR), F32),
-                pltpu.VMEM((length, PAIR), F32),
-                pltpu.VMEM((PAIR, length), F32),
-                pltpu.VMEM((length, D), F32),
-                pltpu.VMEM((4 * CROPS, D), BF16),
-                pltpu.VMEM((2 * CROPS, 2 * D), F32),
-            ],
+            in_specs=[spec for _, spec in back_in[1:]],
+            out_specs=[spec for _, spec in back_out],
+            scratch_shapes=back_temp,
         ),
-        out_shape=[
-            struct((mine, local, D), BF16),
-            struct((far, mine, local, D), BF16),
-            struct((3 * D, D)),
-            struct((1, 3 * D)),
-            struct((mine, CROPS, 2 * D)),
-        ],
+        out_shape=[shape for shape, _ in back_out],
         cost_estimate=pl.CostEstimate(
             flops=2 * tokens_here * (6 * D * D + 5 * D * length),
             transcendentals=0,
             bytes_accessed=20_000_000,
         ),
-    )(
-        place,
-        tokens,
-        tok_in,
-        col,
-        row,
-        modulation,
-        w_qkv,
-        hid,
-        query,
-        key,
-        value,
-        prob,
-        grad_heads,
-        grad_res,
-    )
+    )(*[array for array, _ in back_in])
+    if fast:
+        early_plane, (gt_own, gt_far, *rest) = lax.optimization_barrier(
+            (early_plane, (gt_own, gt_far, *rest))
+        )
+        l_own, l_send, parcel, gml_own, gml_send = rest
+        l_in, gml_in = seq_hop(l_send, 1), seq_hop(gml_send, 1)
+        late = lines + 2 * depth + 8
+        late_keep, *late_sends = glue(
+            late_pack,
+            [struct((outer, late, D))] + [struct((outer, late, D), BF16)] * 3,
+            place,
+            l_own,
+            l_in,
+            gml_own,
+            gml_in,
+            gme_own,
+            gme_in,
+            silu_near,
+            ada_all,
+            slope_t,
+            id_lanes,
+            parcel,
+            temps=[pltpu.VMEM((lanes, 3 * D), BF16), pltpu.VMEM((3 * D, lanes), F32)],
+        )
+        late_plane = [plane_hop(late_sends[k - 1], k) for k in range(1, inner)]
+        keep, *sends = glue(
+            early_line,
+            [struct((early, D))] + [struct((early, D), BF16)] * 3,
+            keep,
+            *early_plane,
+        )
+        early_in = [line_hop(sends[k - 1], k) for k in range(1, outer)]
+        late = late + 24
+        late_keep, *late_sends = glue(
+            late_line,
+            [struct((late, D))] + [struct((late, D), BF16)] * 3,
+            late_keep,
+            *late_plane,
+        )
+        late_in = [line_hop(late_sends[k - 1], k) for k in range(1, outer)]
+        grad_tokens = return_rows(gt_own, gt_far)
+        parts, grad_w_ada = glue(
+            last_pack,
+            [struct((units + lines + 8 * buckets, D)), struct((depth, 3 * D))],
+            place,
+            keep,
+            *early_in,
+            late_keep,
+            *late_in,
+        )
+        table, qkv, qv, proj, bp, fc1, b1, fc2, b2, router, v_ada = glue(
+            finish,
+            [
+                struct((depth, NCLASS)),
+                struct((3 * depth, D)),
+                struct((1, 2 * depth)),
+                struct((depth, D)),
+                struct((1, depth)),
+                struct((units, D)),
+                struct((1, units)),
+                struct((units, D)),
+                struct((1, depth)),
+                struct((1, depth)),
+                struct((1, 3 * depth)),
+            ],
+            place,
+            parts,
+            seq_hop(parts, 1),
+            temps=[
+                pltpu.VMEM((buckets * crops_here, lanes), F32),
+                pltpu.VMEM((buckets * crops_here, 8 * lanes), BF16),
+            ],
+        )
+        return (
+            output,
+            grad_tokens,
+            table.T,
+            grad_w_ada,
+            v_ada,
+            qkv.T,
+            qv.reshape(-1),
+            proj.T,
+            bp.reshape(-1),
+            fc1.T,
+            b1.reshape(-1),
+            fc2,
+            b2.reshape(-1),
+            router.reshape(-1),
+        )
+
+    dw1, dw2, db2, dwr = sums
+    dwq, gmod_first = rest
+    early = sum_over_all([dw1[:, 0:D], dw2])
     grad_tokens = return_rows(gt_own, gt_far)
-    late = sum_over_all([dwq, dwp])
+    late = sum_over_all([dwq[:, 0:D], dwp[:, 0:D]])
 
     grad_mod = jnp.concatenate([gmod_first, gmod_late], -1).astype(BF16).reshape(crops_mine, 6 * D)
     width = 6 * D // seqs
@@ -749,11 +1248,11 @@
         [
             part.reshape(buckets, -1)
             for part in (
-                db1,
-                db2,
-                dbp,
-                dwr,
-                jnp.concatenate([dbq[:, 0:D], dbq[:, 2 * D :]], 1),
+                dw1[:, D],
+                db2[:, 0],
+                dwp[:, D],
+                dwr[:, 0] + dwr[:, lanes // 2],
+                jnp.concatenate([dwq[0:D, D], dwq[2 * D :, D]]),
             )
         ],
         1,

time: 227 us -> 185 us (0.81)
  Pallas kernels: 75.6 us -> 98.9 us
  other arithmetic: 27.8 us -> 5.41 us
  waiting for transfers between devices: 43 us -> 28.3 us
  starting transfers between devices: 41.6 us -> 28.6 us
  local copies, waits for them, and re-layouts: 33.4 us -> 21.2 us
  matrix products: 3.7 us -> 0.58 us
    pallas_call x2 -> x8, Pallas kernels: 75.6 us -> 98.9 us  [the longest x1 56.6 us: body(): pl.pallas_call(partial(forward_kernel, fast), name='layer_forward', grid_...]
    ppermute x15 -> x9, waiting for transfers between devices: 31.9 us -> 19.3 us  [plane_hop(): lax.ppermute(value, 'bucket', [(i, i ^ step) for i in range(buckets)])]
    gather x4 -> x0, local copies, waits for them, and re-layouts: 8.59 us -> none  [the longest x2 7.45 us: sum_over_all(): joined = jnp.take(joined, order, axis=0)]
    ppermute x15 -> x9, starting transfers between devices: 18.4 us -> 10.6 us  [plane_hop(): lax.ppermute(value, 'bucket', [(i, i ^ step) for i in range(buckets)])]
    concatenate x7 -> x1, other arithmetic: 5.99 us -> 0.01 us  [body(): jnp.concatenate([class_ids // 8, class_ids % 8]).astype(F32)[None]]
    select_n x4 -> x1, other arithmetic: 5.11 us -> 0.12 us  [body(): jnp.take(silu_slope.reshape(crops_here, buckets, depth), order, axis=1)]
    ppermute x15 -> x9, starting transfers between devices: 20.8 us -> 16 us  [line_hop(): lax.ppermute(value, 'bucket', [(i, i ^ step * inner) for i in range(bucke...]
    convert_element_type x6 -> x1, other arithmetic: 4.08 us -> 0.08 us  [body(): jnp.concatenate([class_ids // 8, class_ids % 8]).astype(F32)[None]]
  transfers between devices with their start and end apart: 43 -> 29, of which waited for: 22 -> 7; matrix products, arithmetic and copies ran while one was open for 24% -> 12% of each run, Pallas kernels for 10% -> 17%
where the time goes in v2:
time: 185 us; the launch traced here: 184 us
  Pallas kernels  98.9 us (53%)
  starting transfers between devices  28.6 us (15%)
  waiting for transfers between devices  28.3 us (15%)
  local copies, waits for them, and re-layouts  21.2 us (11%)
  other arithmetic  5.41 us (3%)
    pallas_call x1, Pallas kernels, body(): pl.pallas_call(partial(forward_kernel, fast), name='layer_forward', grid_...  56.6 us
    pallas_call x1, Pallas kernels, body(): pl.pallas_call(partial(backward_kernel, fast), name='layer_backward', gri...  25.1 us
    ppermute x9, waiting for transfers between devices, plane_hop(): lax.ppermute(value, 'bucket', [(i, i ^ step) for i in range(buckets)])  19.3 us
    pallas_call x6, Pallas kernels, glue(): pl.pallas_call(kernel, name=kernel.__name__, in_specs=[pl.BlockSpec(memor...  17.2 us
    ppermute x9, starting transfers between devices, line_hop(): lax.ppermute(value, 'bucket', [(i, i ^ step * inner) for i in range(bucke...  16 us
    ppermute x9, starting transfers between devices, plane_hop(): lax.ppermute(value, 'bucket', [(i, i ^ step) for i in range(buckets)])  10.6 us
    unnamed x71, local copies, waits for them, and re-layouts  8.18 us
    ppermute x9, waiting for transfers between devices, line_hop(): lax.ppermute(value, 'bucket', [(i, i ^ step * inner) for i in range(bucke...  6.48 us
  transfers between devices with their start and end apart: 29, of which 7 were waited for; matrix products, arithmetic and copies ran while one was open for 12% of the time, Pallas kernels for 17%

profile of v2, /device:TPU:0, one launch (start us, length us, event | category | flops | bytes accessed | tf_op | source)
XLA Modules:
  0.0 184.5 jit_solution(12677410259275478773)
XLA Ops:
  0.7 3.1 %collective-permute-start.3 = (bf16[24,1152]{1,0:T(8,128)(2,1)}, bf16[24,1152]{1,0:T(8,128)(2,1)S(1)}, u32[]{:S(2)}, u32[]{:S(2)}) collective-permute-start(bf16[24,1152]{1,0:T(8,128)(2,1)} %param.31), channel_id=1, source_target_pairs={{0,8},{2,10},{4,12},{6,14},{8,0},{10,2},{12,4},{14,6},{16,24},{18,... | collective-permute-start | bytes 165896 | tf_op jit(solution)/shard_map/ppermute | solution.py:814
  3.8 2.6 %collective-permute-start.4 = (bf16[24,1152]{1,0:T(8,128)(2,1)}, bf16[24,1152]{1,0:T(8,128)(2,1)S(1)}, u32[]{:S(2)}, u32[]{:S(2)}) collective-permute-start(bf16[24,1152]{1,0:T(8,128)(2,1)} %param.31), channel_id=1, source_target_pairs={{0,16},{2,18},{4,20},{6,22},{8,24},{10,26},{12,28},{14,30},{16,0},... | collective-permute-start | bytes 165896 | tf_op jit(solution)/shard_map/ppermute | solution.py:814
  8.8 1.4 constant_dynamic-update-slice_fusion.3
  16.8 1.7 collective-permute-start.6
  24.0 1.6 collective-permute-start.7
  25.8 10.7 %collective-permute-done.7 = bf16[96,1152]{1,0:T(8,128)(2,1)S(1)} collective-permute-done((bf16[96,1152]{1,0:T(8,128)(2,1)}, bf16[96,1152]{1,0:T(8,128)(2,1)S(1)}, u32[]{:S(2)}, u32[]{:S(2)}) %collective-permute-start.7) | collective-permute-done | bytes 221216 | tf_op jit(solution)/shard_map/ppermute | solution.py:811
  39.7 56.6 %layer_forward.1 = (bf16[2,256,384]{2,1,0:T(8,128)(2,1)}, bf16[1,2,256,384]{3,2,1,0:T(8,128)(2,1)}, bf16[2,512,384]{2,1,0:T(8,128)(2,1)}, bf16[2,512,384]{2,1,0:...) custom-call(s32[2]{0:T(128)} %pad_add_fusion.refs_0_.place, ...), custom_call_target="tpu_custom_call" | custom-call | flops 9261023232 | bytes 20000000 | tf_op jit(solution)/shard_map/layer_forward/pallas_call | solution.py:955
  97.6 1.9 %collective-permute-done.12.gm_in.gme_in = f32[2,8,384]{2,1,0:T(8,128)S(1)} collective-permute-done((f32[2,8,384]{2,1,0:T(8,128)}, f32[2,8,384]{2,1,0:T(8,128)S(1)}, u32[]{:S(2)}, u32[]{:S(2)}) %collective-permute-start.12) | collective-permute-done | bytes 24608 | tf_op jit(solution)/shard_map/ppermute | solution.py:808
  100.5 3.5 %early_pack.1 = (f32[4,120,384]{2,1,0:T(8,128)}, bf16[4,120,384]{2,1,0:T(8,128)(2,1)}, bf16[4,120,384]{2,1,0:T(8,128)(2,1)}, bf16[4,120,384]{2,1,0:T(8,128)(2,1)}) custom-call(s32[2]{0:T(128)} %pad_add_fusion.refs_0_.place, f32[16,96,384]{2,1,0:T(8,128)} %get-tuple-element.80.e_own, bf16[16,96,384]{2,1,0:T(8,128)(2,1)} %copy-done.2, ...), custom_call_target="tpu_custom_call" | custom-call | bytes 6000000 | tf_op jit(solution)/shard_map/early_pack/pallas_call | solution.py:1042
  104.4 1.7 collective-permute-start.14
  107.6 25.1 %layer_backward.1 = (bf16[2,256,384]{2,1,0:T(8,128)(2,1)}, bf16[1,2,256,384]{3,2,1,0:T(8,128)(2,1)}, f32[16,48,384]{2,1,0:T(8,128)}, bf16[16,48,384]{2,1,0:T(8,1...) custom-call(s32[2]{0:T(128)} %pad_add_fusion.refs_0_.place, ...), custom_call_target="tpu_custom_call" | custom-call | flops 3825205248 | bytes 20000000 | tf_op jit(solution)/shard_map/layer_backward/pallas_call | solution.py:1119
  137.3 4.2 %late_pack.1 = (f32[4,104,384]{2,1,0:T(8,128)}, bf16[4,104,384]{2,1,0:T(8,128)(2,1)}, bf16[4,104,384]{2,1,0:T(8,128)(2,1)}, bf16[4,104,384]{2,1,0:T(8,128)(2,1)}) custom-call(s32[2]{0:T(128)} %pad_add_fusion.refs_0_.place, f32[16,48,384]{2,1,0:T(8,128)} %get-tuple-element.116.l_own, bf16[16,48,384]{2,1,0:T(8,128)(2,1)} %copy-done.3, ...), custom_call_target="tpu_custom_call" | custom-call | bytes 6000000 | tf_op jit(solution)/shard_map/late_pack/pallas_call | solution.py:1042
  141.9 1.7 collective-permute-start.23
  143.6 1.4 collective-permute-start.24
  145.0 2.2 %early_line.1 = (f32[120,384]{1,0:T(8,128)}, bf16[120,384]{1,0:T(8,128)(2,1)}, bf16[120,384]{1,0:T(8,128)(2,1)}, bf16[120,384]{1,0:T(8,128)(2,1)}) custom-call(f32[4,120,384]{2,1,0:T(8,128)} %get-tuple-element.108.own, bf16[4,120,384]{2,1,0:T(8,128)(2,1)} %copy-done.8, bf16[4,120,384]{2,1,0:T(8,128)(2,1)} %copy-done.9, bf16[4,120,384]{2,1,0:T(8,128)(2,1)} %copy-done.10), custom_call_target="tpu_custom_call" | custom-call | bytes 6000000 | tf_op jit(solution)/shard_map/early_line/pallas_call | solution.py:1042
  147.9 4.2 %collective-permute-done.22.in1 = bf16[4,104,384]{2,1,0:T(8,128)(2,1)S(1)} collective-permute-done((bf16[4,104,384]{2,1,0:T(8,128)(2,1)}, bf16[4,104,384]{2,1,0:T(8,128)(2,1)S(1)}, u32[]{:S(2)}, u32[]{:S(2)}) %collective-permute-start.22) | collective-permute-done | bytes 319520 | tf_op jit(solution)/shard_map/ppermute | solution.py:811
  152.1 1.7 collective-permute-start.18
  153.8 4.4 %collective-permute-done.23.in2 = bf16[4,104,384]{2,1,0:T(8,128)(2,1)S(1)} collective-permute-done((bf16[4,104,384]{2,1,0:T(8,128)(2,1)}, bf16[4,104,384]{2,1,0:T(8,128)(2,1)S(1)}, u32[]{:S(2)}, u32[]{:S(2)}) %collective-permute-start.23) | collective-permute-done | bytes 319520 | tf_op jit(solution)/shard_map/ppermute | solution.py:811
  158.2 3.6 %collective-permute-start.19 = (bf16[120,384]{1,0:T(8,128)(2,1)}, bf16[120,384]{1,0:T(8,128)(2,1)S(1)}, u32[]{:S(2)}, u32[]{:S(2)}) collective-permute-start(bf16[120,384]{1,0:T(8,128)(2,1)} %get-tuple-element.115), channel_id=1, source_target_pairs={{0,24},{2,26},{4,28},{6,30},{8,16},{10,18},{12,20},{14,22},{16,8},... | collective-permute-start | bytes 276488 | tf_op jit(solution)/shard_map/ppermute | solution.py:814
  162.5 2.2 %late_line.1 = (f32[128,384]{1,0:T(8,128)}, bf16[128,384]{1,0:T(8,128)(2,1)}, bf16[128,384]{1,0:T(8,128)(2,1)}, bf16[128,384]{1,0:T(8,128)(2,1)}) custom-call(f32[4,104,384]{2,1,0:T(8,128)} %get-tuple-element.121.own, bf16[4,104,384]{2,1,0:T(8,128)(2,1)} %copy-done.11, bf16[4,104,384]{2,1,0:T(8,128)(2,1)} %copy-done.12, bf16[4,104,384]{2,1,0:T(8,128)(2,1)} %copy-done.13), custom_call_target="tpu_custom_call" | custom-call | bytes 6000000 | tf_op jit(solution)/shard_map/late_line/pallas_call | solution.py:1042
  166.2 3.0 %collective-permute-start.27 = (bf16[128,384]{1,0:T(8,128)(2,1)}, bf16[128,384]{1,0:T(8,128)(2,1)S(1)}, u32[]{:S(2)}, u32[]{:S(2)}) collective-permute-start(bf16[128,384]{1,0:T(8,128)(2,1)} %get-tuple-element.128), channel_id=1, source_target_pairs={{0,24},{2,26},{4,28},{6,30},{8,16},{10,18},{12,20},{14,22},{16,8},... | collective-permute-start | bytes 294920 | tf_op jit(solution)/shard_map/ppermute | solution.py:814
  170.5 5.2 %collective-permute-done.26.l2 = bf16[128,384]{1,0:T(8,128)(2,1)S(1)} collective-permute-done((bf16[128,384]{1,0:T(8,128)(2,1)}, bf16[128,384]{1,0:T(8,128)(2,1)S(1)}, u32[]{:S(2)}, u32[]{:S(2)}) %collective-permute-start.26) | collective-permute-done | bytes 98336 | tf_op jit(solution)/shard_map/ppermute | solution.py:814
  176.4 2.1 %last_pack.1 = (f32[272,384]{1,0:T(8,128)}, f32[24,1152]{1,0:T(8,128)}) custom-call(s32[2]{0:T(128)} %pad_add_fusion.refs_0_.place, f32[120,384]{1,0:T(8,128)} %get-tuple-element.112.early, bf16[120,384]{1,0:T(8,128)(2,1)} %copy-done.18, bf16[120,384]{1,0:T(8,128)(2,1)} %copy-done.19, bf16[120,384]{1,0:T(8,128)(2,1)} %copy-done.20, ...), custom_call_target="tpu_custom_call" | custom-call | bytes 6000000 | tf_op jit(solution)/shard_map/last_pack/pallas_call | solution.py:1042
  181.3 2.9 %finish.1 = (f32[24,1000]{1,0:T(8,128)}, f32[72,384]{1,0:T(8,128)}, f32[1,48]{1,0:T(1,128)}, f32[24,384]{1,0:T(8,128)}, f32[1,24]{1,0:T(1,128)}, /*index=5*/f32[...) custom-call(s32[2]{0:T(128)} %pad_add_fusion.refs_0_.place, ...), custom_call_target="tpu_custom_call" | custom-call | bytes 6000000 | tf_op jit(solution)/shard_map/finish/pallas_call | solution.py:1042
  (175 shorter events, 34.2 us)
Async XLA Ops:
  0.7 14.1 %collective-permute-start.3 = (bf16[24,1152]{1,0:T(8,128)(2,1)}, bf16[24,1152]{1,0:T(8,128)(2,1)S(1)}, u32[]{:S(2)}, u32[]{:S(2)}) collective-permute-start(bf16[24,1152]{1,0:T(8,128)(2,1)} %param.31), channel_id=1, source_target_pairs={{0,8},{2,10},{4,12},{6,14},{8,0},{10,2},{12,4},{14,6},{16,24},{18,... | collective-permute-start | bytes 165896 | tf_op jit(solution)/shard_map/ppermute | solution.py:814
  3.8 11.8 %collective-permute-start.4 = (bf16[24,1152]{1,0:T(8,128)(2,1)}, bf16[24,1152]{1,0:T(8,128)(2,1)S(1)}, u32[]{:S(2)}, u32[]{:S(2)}) collective-permute-start(bf16[24,1152]{1,0:T(8,128)(2,1)} %param.31), channel_id=1, source_target_pairs={{0,16},{2,18},{4,20},{6,22},{8,24},{10,26},{12,28},{14,30},{16,0},... | collective-permute-start | bytes 165896 | tf_op jit(solution)/shard_map/ppermute | solution.py:814
  6.4 9.8 %collective-permute-start.5 = (bf16[24,1152]{1,0:T(8,128)(2,1)}, bf16[24,1152]{1,0:T(8,128)(2,1)S(1)}, u32[]{:S(2)}, u32[]{:S(2)}) collective-permute-start(bf16[24,1152]{1,0:T(8,128)(2,1)} %param.31), channel_id=1, source_target_pairs={{0,24},{2,26},{4,28},{6,30},{8,16},{10,18},{12,20},{14,22},{16,8},... | collective-permute-start | bytes 165896 | tf_op jit(solution)/shard_map/ppermute | solution.py:814
  7.1 16.8 %collective-permute-start.2 = (s32[2,256]{1,0:T(2,128)S(1)}, s32[2,256]{1,0:T(2,128)S(1)}, u32[]{:S(2)}, u32[]{:S(2)}) collective-permute-start(s32[2,256]{1,0:T(2,128)S(1)} %get-tuple-element.163), channel_id=1, source_target_pairs={{0,1},{1,0},{2,3},{3,2},{4,5},{5,4},{6,7},{7,6},{8,9},{9,8},{10,11... | collective-permute-start | bytes 6152 | tf_op jit(solution)/shard_map/ppermute | solution.py:808
  8.2 30.8 %collective-permute-start = (bf16[2,256,384]{2,1,0:T(8,128)(2,1)S(1)}, bf16[2,256,384]{2,1,0:T(8,128)(2,1)S(1)}, u32[]{:S(2)}, u32[]{:S(2)}) collective-permute-start(bf16[2,256,384]{2,1,0:T(8,128)(2,1)S(1)} %constant_dynamic-slice_fusion.6), channel_id=1, source_target_pairs={{0,1},{1,0},{2,3},{3,2},{4,5},{5,4},{6,7},{7,6},{8,9},{9,8},{10,11... | collective-permute-start | bytes 1179656 | tf_op jit(solution)/shard_map/ppermute | solution.py:808
  14.8 24.1 %collective-permute-start.1 = (bf16[2,256,384]{2,1,0:T(8,128)(2,1)S(1)}, bf16[2,256,384]{2,1,0:T(8,128)(2,1)}, u32[]{:S(2)}, u32[]{:S(2)}) collective-permute-start(bf16[2,256,384]{2,1,0:T(8,128)(2,1)S(1)} %constant_dynamic-slice_fusion.5), channel_id=1, source_target_pairs={{0,1},{1,0},{2,3},{3,2},{4,5},{5,4},{6,7},{7,6},{8,9},{9,8},{10,11... | collective-permute-start | bytes 1179656 | tf_op jit(solution)/shard_map/ppermute | solution.py:808
  16.8 9.0 %collective-permute-start.6 = (bf16[96,1152]{1,0:T(8,128)(2,1)}, bf16[96,1152]{1,0:T(8,128)(2,1)S(1)}, u32[]{:S(2)}, u32[]{:S(2)}) collective-permute-start(bf16[96,1152]{1,0:T(8,128)(2,1)} %get-tuple-element.148), channel_id=1, source_target_pairs={{0,2},{2,0},{4,6},{6,4},{8,10},{10,8},{12,14},{14,12},{16,18},{18,... | collective-permute-start | bytes 663560 | tf_op jit(solution)/shard_map/ppermute | solution.py:811
  24.0 12.6 %collective-permute-start.7 = (bf16[96,1152]{1,0:T(8,128)(2,1)}, bf16[96,1152]{1,0:T(8,128)(2,1)S(1)}, u32[]{:S(2)}, u32[]{:S(2)}) collective-permute-start(bf16[96,1152]{1,0:T(8,128)(2,1)} %get-tuple-element.148), channel_id=1, source_target_pairs={{0,4},{2,6},{4,0},{6,2},{8,12},{10,14},{12,8},{14,10},{16,20},{18,... | collective-permute-start | bytes 663560 | tf_op jit(solution)/shard_map/ppermute | solution.py:811
  25.6 11.0 %collective-permute-start.8 = (bf16[96,1152]{1,0:T(8,128)(2,1)}, bf16[96,1152]{1,0:T(8,128)(2,1)S(1)}, u32[]{:S(2)}, u32[]{:S(2)}) collective-permute-start(bf16[96,1152]{1,0:T(8,128)(2,1)} %get-tuple-element.148), channel_id=1, source_target_pairs={{0,6},{2,4},{4,2},{6,0},{8,14},{10,12},{12,10},{14,8},{16,22},{18,... | collective-permute-start | bytes 663560 | tf_op jit(solution)/shard_map/ppermute | solution.py:811
  96.3 3.2 %collective-permute-start.11 = (bf16[16,96,384]{2,1,0:T(8,128)(2,1)}, bf16[16,96,384]{2,1,0:T(8,128)(2,1)S(1)}, u32[]{:S(2)}, u32[]{:S(2)}) collective-permute-start(bf16[16,96,384]{2,1,0:T(8,128)(2,1)} %get-tuple-element.81), channel_id=1, source_target_pairs={{0,1},{1,0},{2,3},{3,2},{4,5},{5,4},{6,7},{7,6},{8,9},{9,8},{10,11... | collective-permute-start | bytes 3538952 | tf_op jit(solution)/shard_map/ppermute | solution.py:808
  104.1 28.7 %collective-permute-start.13 = (bf16[4,120,384]{2,1,0:T(8,128)(2,1)}, bf16[4,120,384]{2,1,0:T(8,128)(2,1)S(1)}, u32[]{:S(2)}, u32[]{:S(2)}) collective-permute-start(bf16[4,120,384]{2,1,0:T(8,128)(2,1)} %get-tuple-element.84), channel_id=1, source_target_pairs={{0,2},{2,0},{4,6},{6,4},{8,10},{10,8},{12,14},{14,12},{16,18},{18,... | collective-permute-start | bytes 1105928 | tf_op jit(solution)/shard_map/ppermute | solution.py:811
  104.4 28.3 %collective-permute-start.14 = (bf16[4,120,384]{2,1,0:T(8,128)(2,1)}, bf16[4,120,384]{2,1,0:T(8,128)(2,1)S(1)}, u32[]{:S(2)}, u32[]{:S(2)}) collective-permute-start(bf16[4,120,384]{2,1,0:T(8,128)(2,1)} %get-tuple-element.85), channel_id=1, source_target_pairs={{0,4},{2,6},{4,0},{6,2},{8,12},{10,14},{12,8},{14,10},{16,20},{18,... | collective-permute-start | bytes 1105928 | tf_op jit(solution)/shard_map/ppermute | solution.py:811
  106.1 26.6 %collective-permute-start.15 = (bf16[4,120,384]{2,1,0:T(8,128)(2,1)}, bf16[4,120,384]{2,1,0:T(8,128)(2,1)S(1)}, u32[]{:S(2)}, u32[]{:S(2)}) collective-permute-start(bf16[4,120,384]{2,1,0:T(8,128)(2,1)} %get-tuple-element.86), channel_id=1, source_target_pairs={{0,6},{2,4},{4,2},{6,0},{8,14},{10,12},{12,10},{14,8},{16,22},{18,... | collective-permute-start | bytes 1105928 | tf_op jit(solution)/shard_map/ppermute | solution.py:811
  141.5 10.7 %collective-permute-start.22 = (bf16[4,104,384]{2,1,0:T(8,128)(2,1)}, bf16[4,104,384]{2,1,0:T(8,128)(2,1)S(1)}, u32[]{:S(2)}, u32[]{:S(2)}) collective-permute-start(bf16[4,104,384]{2,1,0:T(8,128)(2,1)} %get-tuple-element.122), channel_id=1, source_target_pairs={{0,2},{2,0},{4,6},{6,4},{8,10},{10,8},{12,14},{14,12},{16,18},{18,... | collective-permute-start | bytes 958472 | tf_op jit(solution)/shard_map/ppermute | solution.py:811
  141.9 22.9 %collective-permute-start.10 = (bf16[2,256,384]{2,1,0:T(8,128)(2,1)}, bf16[2,256,384]{2,1,0:T(8,128)(2,1)S(1)}, u32[]{:S(2)}, u32[]{:S(2)}) collective-permute-start(bf16[2,256,384]{2,1,0:T(8,128)(2,1)} %bitcast.11), channel_id=1, source_target_pairs={{0,1},{1,0},{2,3},{3,2},{4,5},{5,4},{6,7},{7,6},{8,9},{9,8},{10,11... | collective-permute-start | bytes 1179656 | tf_op jit(solution)/shard_map/ppermute | solution.py:808
  141.9 16.4 %collective-permute-start.23 = (bf16[4,104,384]{2,1,0:T(8,128)(2,1)}, bf16[4,104,384]{2,1,0:T(8,128)(2,1)S(1)}, u32[]{:S(2)}, u32[]{:S(2)}) collective-permute-start(bf16[4,104,384]{2,1,0:T(8,128)(2,1)} %get-tuple-element.123), channel_id=1, source_target_pairs={{0,4},{2,6},{4,0},{6,2},{8,12},{10,14},{12,8},{14,10},{16,20},{18,... | collective-permute-start | bytes 958472 | tf_op jit(solution)/shard_map/ppermute | solution.py:811
  143.6 18.2 %collective-permute-start.24 = (bf16[4,104,384]{2,1,0:T(8,128)(2,1)}, bf16[4,104,384]{2,1,0:T(8,128)(2,1)S(1)}, u32[]{:S(2)}, u32[]{:S(2)}) collective-permute-start(bf16[4,104,384]{2,1,0:T(8,128)(2,1)} %get-tuple-element.124), channel_id=1, source_target_pairs={{0,6},{2,4},{4,2},{6,0},{8,14},{10,12},{12,10},{14,8},{16,22},{18,... | collective-permute-start | bytes 958472 | tf_op jit(solution)/shard_map/ppermute | solution.py:811
  147.3 17.5 %collective-permute-start.17 = (bf16[120,384]{1,0:T(8,128)(2,1)}, bf16[120,384]{1,0:T(8,128)(2,1)S(1)}, u32[]{:S(2)}, u32[]{:S(2)}) collective-permute-start(bf16[120,384]{1,0:T(8,128)(2,1)} %get-tuple-element.113), channel_id=1, source_target_pairs={{0,8},{2,10},{4,12},{6,14},{8,0},{10,2},{12,4},{14,6},{16,24},{18,... | collective-permute-start | bytes 276488 | tf_op jit(solution)/shard_map/ppermute | solution.py:814
  152.1 14.0 %collective-permute-start.18 = (bf16[120,384]{1,0:T(8,128)(2,1)}, bf16[120,384]{1,0:T(8,128)(2,1)S(1)}, u32[]{:S(2)}, u32[]{:S(2)}) collective-permute-start(bf16[120,384]{1,0:T(8,128)(2,1)} %get-tuple-element.114), channel_id=1, source_target_pairs={{0,16},{2,18},{4,20},{6,22},{8,24},{10,26},{12,28},{14,30},{16,0},... | collective-permute-start | bytes 276488 | tf_op jit(solution)/shard_map/ppermute | solution.py:814
  158.2 11.0 %collective-permute-start.19 = (bf16[120,384]{1,0:T(8,128)(2,1)}, bf16[120,384]{1,0:T(8,128)(2,1)S(1)}, u32[]{:S(2)}, u32[]{:S(2)}) collective-permute-start(bf16[120,384]{1,0:T(8,128)(2,1)} %get-tuple-element.115), channel_id=1, source_target_pairs={{0,24},{2,26},{4,28},{6,30},{8,16},{10,18},{12,20},{14,22},{16,8},... | collective-permute-start | bytes 276488 | tf_op jit(solution)/shard_map/ppermute | solution.py:814
  161.8 17.7 %collective-permute-start.16 = (bf16[2,256,384]{2,1,0:T(8,128)(2,1)}, bf16[2,256,384]{2,1,0:T(8,128)(2,1)S(1)}, u32[]{:S(2)}, u32[]{:S(2)}) collective-permute-start(bf16[2,256,384]{2,1,0:T(8,128)(2,1)} %bitcast.48), channel_id=1, source_target_pairs={{0,1},{1,0},{2,3},{3,2},{4,5},{5,4},{6,7},{7,6},{8,9},{9,8},{10,11... | collective-permute-start | bytes 1179656 | tf_op jit(solution)/shard_map/ppermute | solution.py:808
  164.7 5.8 %collective-permute-start.25 = (bf16[128,384]{1,0:T(8,128)(2,1)}, bf16[128,384]{1,0:T(8,128)(2,1)S(1)}, u32[]{:S(2)}, u32[]{:S(2)}) collective-permute-start(bf16[128,384]{1,0:T(8,128)(2,1)} %get-tuple-element.126), channel_id=1, source_target_pairs={{0,8},{2,10},{4,12},{6,14},{8,0},{10,2},{12,4},{14,6},{16,24},{18,... | collective-permute-start | bytes 294920 | tf_op jit(solution)/shard_map/ppermute | solution.py:814
  164.8 10.9 %collective-permute-start.26 = (bf16[128,384]{1,0:T(8,128)(2,1)}, bf16[128,384]{1,0:T(8,128)(2,1)S(1)}, u32[]{:S(2)}, u32[]{:S(2)}) collective-permute-start(bf16[128,384]{1,0:T(8,128)(2,1)} %get-tuple-element.127), channel_id=1, source_target_pairs={{0,16},{2,18},{4,20},{6,22},{8,24},{10,26},{12,28},{14,30},{16,0},... | collective-permute-start | bytes 294920 | tf_op jit(solution)/shard_map/ppermute | solution.py:814
  166.2 9.6 %collective-permute-start.27 = (bf16[128,384]{1,0:T(8,128)(2,1)}, bf16[128,384]{1,0:T(8,128)(2,1)S(1)}, u32[]{:S(2)}, u32[]{:S(2)}) collective-permute-start(bf16[128,384]{1,0:T(8,128)(2,1)} %get-tuple-element.128), channel_id=1, source_target_pairs={{0,24},{2,26},{4,28},{6,30},{8,16},{10,18},{12,20},{14,22},{16,8},... | collective-permute-start | bytes 294920 | tf_op jit(solution)/shard_map/ppermute | solution.py:814
  (38 other events, 273.2 us)
